TPU v7x, 512 devices: a whole 4x4x16 slice. The times are simulated.
512 devices in a mesh: gx: 32 (over y, x, core), gy: 16 (over z).
Axes of the slice: x: 4, y: 4, z: 16, core: 2. Of those that a mesh axis runs over, the one named last changes fastest.
Arguments:
- right_side: float32 [3, 128, 64, 128], P(None, 'gx', 'gy'), may hold values from -10 to 10
- node_mass: float32 [128, 64, 128], P('gx', 'gy'), may hold values from 0.5 to 4
- gradients: float32 [32, 16, 8, 3, 27, 128], P('gx', 'gy'), may hold values from -3 to 3
- stiffness: float32 [32, 16, 8, 128], P('gx', 'gy'), may hold values from 0.2 to 2
- valid: int32 [32, 16, 8, 128], P('gx', 'gy'), may hold values 0 or 1
- node_base: int32 [32, 16, 8, 128], P('gx', 'gy'), may hold values from 0 to 2857, as said below
Outputs:
- solution: float32 [3, 128, 64, 128], P(None, 'gx', 'gy')
- residual: float32 [3, 128, 64, 128], P(None, 'gx', 'gy')
Inputs may be any that keep to these rules, and one draw needn't show every extreme that they name: node_base = (i * 6 + j) * 130 + k with 0 <= i < 4, 0 <= j < 4, 0 <= k < 128.
All inputs are finite; a program needn't handle non-finite values. No bound on the sum of `valid` on one device may be relied on, other than what follows from the above.
Results may differ from a plain program's by a relative error of at most 0.00011.
Values sent between devices are 32-bit elements; how exact they have to be, the bound alone decides.
A program may use at most 64 MiB of HBM per device.

v0:
```python
import functools

import jax
import jax.numpy as jnp
from jax import lax
from jax.sharding import Mesh
from jax.sharding import PartitionSpec as P

ITERS = 2
SWEEPS = 4
GX_GY = ("gx_0", "gx_1", "gx_2", "gy")
GX = ("gx_0", "gx_1", "gx_2")


POISSON = 0.3
DAMPING = 0.7
LAPLACE_WEIGHT = 1.0


def extended(array, sides, width):
    edges = {}
    for axis, dim in sides:
        count, length = (lax.axis_size(axis), array.shape[dim])
        up = [(i, (i + 1) % count) for i in range(count - 1)]
        last = lax.slice_in_dim(array, length - width, length, axis=dim)
        leading = lax.slice_in_dim(array, 0, width, axis=dim)
        edges[dim] = (
            lax.ppermute(last, axis, up),
            lax.ppermute(leading, axis, [(b, a) for a, b in up]),
        )
    done = []
    for _, dim in sides:
        low, high = edges[dim]
        around = [(width, width) if d in done else (0, 0) for d in range(array.ndim)]
        array = jnp.concatenate([jnp.pad(low, around), array, jnp.pad(high, around)], axis=dim)
        done.append(dim)
    return array


def padded_2(array, sides, width):
    for axis, dim in sides:
        count, length = (lax.axis_size(axis), array.shape[dim])
        up = [(i, (i + 1) % count) for i in range(count - 1)]
        down = [(j, i) for i, j in up]
        last = lax.slice_in_dim(array, length - width, length, axis=dim)
        leading = lax.slice_in_dim(array, 0, width, axis=dim)
        before = lax.ppermute(last, axis, up)
        after = lax.ppermute(leading, axis, down)
        array = jnp.concatenate([before, array, after], axis=dim)
    return array


def over_axes(array, axes):
    return functools.reduce(lax.psum, axes, array)


def particle_forces(values, gradients, stiffness):
    grad_disp = jnp.einsum(
        "...inp,...jnp->...ijp", values, gradients, precision=lax.Precision.HIGHEST
    )
    strain_trace = grad_disp[..., 0, 0, :] + grad_disp[..., 1, 1, :] + grad_disp[..., 2, 2, :]
    first_lame = stiffness * (POISSON / ((1.0 + POISSON) * (1.0 - 2.0 * POISSON)))
    shear_mod = stiffness * (0.5 / (1.0 + POISSON))
    identity = jnp.eye(3, dtype=values.dtype).reshape(3, 3, 1)
    stress = shear_mod[..., None, None, :] * (grad_disp + jnp.swapaxes(grad_disp, -3, -2))
    stress = stress + identity * (first_lame * strain_trace)[..., None, None, :]
    return jnp.einsum("...ijp,...jnp->...inp", stress, gradients, precision=lax.Precision.HIGHEST)


def grid_from_padded(padded, mass_diag, coupling):
    center = padded[:, 1:-1, 1:-1, 1:-1]
    beside = padded[:, 2:, 1:-1, 1:-1] + padded[:, :-2, 1:-1, 1:-1]
    beside = beside + padded[:, 1:-1, 2:, 1:-1] + padded[:, 1:-1, :-2, 1:-1]
    beside = beside + padded[:, 1:-1, 1:-1, 2:] + padded[:, 1:-1, 1:-1, :-2]
    return mass_diag * center + coupling * (6.0 * center - beside)


def grid_local(nodal, mass_diag, coupling):
    rimmed = extended(nodal, ((GX, 1), ("gy", 2)), 1)
    return grid_from_padded(jnp.pad(rimmed, ((0, 0), (0, 0), (0, 0), (1, 1))), mass_diag, coupling)


def grid_coarse(nodal, mass_diag, coupling):
    rimmed = extended(nodal, ((GX, 1), ("gy", 2)), 1)
    return grid_from_padded(jnp.pad(rimmed, ((0, 0), (0, 0), (0, 0), (1, 1))), mass_diag, coupling)


def aggregate(nodal):
    dims_in = nodal.shape
    leading = dims_in[:-3]
    blocked = nodal.reshape(
        leading + (dims_in[-3] // 2, 2, dims_in[-2] // 2, 2, dims_in[-1] // 2, 2)
    )
    return blocked.sum(axis=(-5, -3, -1))


def expand(nodal):
    return jnp.repeat(jnp.repeat(jnp.repeat(nodal, 2, axis=-3), 2, axis=-2), 2, axis=-1)


def coarse_sweeps(source, mass_diag, coupling, apply_fn):
    diagonal = mass_diag + 6.0 * coupling
    estimate = DAMPING * source / diagonal
    for sweep_index in range(SWEEPS - 1):
        estimate = (
            estimate + DAMPING * (source - apply_fn(estimate, mass_diag, coupling)) / diagonal
        )
    return estimate


def vcycle(source, masses, depth_index, whole_mass):
    mass_diag = masses[depth_index]
    coupling = LAPLACE_WEIGHT * 2.0**depth_index
    if depth_index == 2:
        return coarse_sweeps(source, mass_diag, coupling, grid_coarse)
    diagonal = mass_diag + 6.0 * coupling
    estimate = DAMPING * source / diagonal
    remainder = source - grid_local(estimate, mass_diag, coupling)
    estimate = estimate + expand(vcycle(aggregate(remainder), masses, depth_index + 1, whole_mass))
    return estimate + DAMPING * (source - grid_local(estimate, mass_diag, coupling)) / diagonal


def compact_bases(node_base, rows_y, rows_z):
    local_z = node_base % (rows_z + 2)
    quotient = node_base // (rows_z + 2)
    local_y = quotient % (rows_y + 2)
    local_x = quotient // (rows_y + 2)
    return (local_x * rows_y + local_y) * rows_z + local_z


def stiffness_local(nodal, gradients, effective, compact):
    rows_x = nodal.shape[1]
    rows_y = nodal.shape[2]
    rows_z = nodal.shape[3]
    node_count = rows_x * rows_y * rows_z
    rimmed = padded_2(nodal, ((GX, 1), ("gy", 2)), 1)
    padded = jnp.pad(rimmed, ((0, 0), (0, 0), (0, 0), (1, 1)))
    shifted = []
    for tile_pos in range(27):
        off_a = tile_pos // 9
        off_b = tile_pos // 3 % 3
        off_c = tile_pos % 3
        window = padded[:, off_a : off_a + rows_x, off_b : off_b + rows_y, off_c : off_c + rows_z]
        shifted.append(window.reshape(3, node_count))
    stacked = jnp.stack(shifted, axis=0).reshape(81, node_count)
    node_iota = jnp.arange(node_count, dtype=jnp.int32)

    def per_block(accumulated, block):
        grad_blk, stiff_blk, base_blk = block
        one_hot = (base_blk[:, None] == node_iota[None, :]).astype(jnp.float32)
        picked = lax.dot_general(
            stacked,
            one_hot,
            (((1,), (1,)), ((), ())),
            precision=lax.Precision.HIGHEST,
            preferred_element_type=jnp.float32,
        )
        values = jnp.swapaxes(picked.reshape(27, 3, -1), 0, 1)
        forces = particle_forces(values, grad_blk, stiff_blk)
        force_rows = jnp.swapaxes(forces, 0, 1).reshape(81, -1)
        accumulated = accumulated + jnp.dot(
            force_rows, one_hot, precision=lax.Precision.HIGHEST, preferred_element_type=jnp.float32
        )
        return (accumulated, None)

    initial = jnp.zeros((81, node_count), jnp.float32)
    summed, unused = lax.scan(per_block, initial, (gradients, effective, compact))
    summed = summed.reshape(27, 3, rows_x, rows_y, rows_z)
    spread = jnp.zeros((3, rows_x + 2, rows_y + 2, rows_z + 2), jnp.float32)
    for tile_pos in range(27):
        off_a = tile_pos // 9
        off_b = tile_pos // 3 % 3
        off_c = tile_pos % 3
        spread = spread.at[
            :, off_a : off_a + rows_x, off_b : off_b + rows_y, off_c : off_c + rows_z
        ].add(summed[tile_pos])
    spread = spread[..., 1:-1]
    rim_pair = jnp.concatenate((spread[:, :1], spread[:, rows_x + 1 :]), axis=1)
    received = padded_2(rim_pair, ((GX, 1),), 1)
    inner_part = spread[:, 1 : rows_x + 1]
    inner_part = inner_part.at[:, 0].add(received[:, 0]).at[:, rows_x - 1].add(received[:, 3])
    rim_pair = jnp.concatenate((inner_part[:, :, :1], inner_part[:, :, rows_y + 1 :]), axis=2)
    received = padded_2(rim_pair, (("gy", 2),), 1)
    inner_part = inner_part[:, :, 1 : rows_y + 1]
    return inner_part.at[:, :, 0].add(received[:, :, 0]).at[:, :, rows_y - 1].add(received[:, :, 3])


def both_inner(residual, precond, applied):
    return (
        over_axes(jnp.sum(residual * precond), GX_GY),
        over_axes(jnp.sum(applied * precond), GX_GY),
    )


def per_device(right_side, node_mass, gradients, stiffness, valid, node_base):
    grads_local = gradients[0, 0]
    effective = stiffness[0, 0] * valid[0, 0].astype(jnp.float32)
    compact = compact_bases(node_base[0, 0], right_side.shape[2], right_side.shape[3])
    masses = [node_mass, aggregate(node_mass), aggregate(aggregate(node_mass))]
    whole_mass = None

    def operator(nodal):
        return node_mass * nodal + stiffness_local(nodal, grads_local, effective, compact)

    def precondition(nodal):
        return vcycle(nodal, masses, 0, whole_mass)

    solution = jnp.zeros_like(right_side)
    residual = right_side
    precond = precondition(residual)
    applied = operator(precond)
    inner_now, curvature_sum = both_inner(residual, precond, applied)
    step_size = inner_now / curvature_sum
    direction = precond
    applied_dir = applied
    for iteration in range(ITERS):
        solution = solution + step_size * direction
        residual = residual - step_size * applied_dir
        if iteration + 1 < ITERS:
            precond = precondition(residual)
            applied = operator(precond)
            inner_next, curvature_sum = both_inner(residual, precond, applied)
            ratio_next = inner_next / inner_now
            step_size = inner_next / (curvature_sum - ratio_next * inner_next / step_size)
            direction = precond + ratio_next * direction
            applied_dir = applied + ratio_next * applied_dir
            inner_now = inner_next
    return (solution, residual)


def solution(mesh):
    finer = Mesh(mesh.devices.reshape(4, 4, 2, mesh.shape["gy"]), ("gx_0", "gx_1", "gx_2", "gy"))
    in_specs = (
        P(None, GX, "gy", None),
        P(GX, "gy", None),
        P(GX, "gy", None, None, None, None),
        P(GX, "gy", None, None),
        P(GX, "gy", None, None),
        P(GX, "gy", None, None),
    )
    out_specs = (P(None, GX, "gy", None), P(None, GX, "gy", None))
    return jax.shard_map(
        per_device, mesh=finer, in_specs=in_specs, out_specs=out_specs, check_vma=False
    )
```

profile of v0, /device:TPU:2, one launch (start us, length us, event | category | flops | bytes accessed | tf_op | source)
XLA Modules:
  0.0 732.7 jit_solution(5629486326822065015)
XLA Ops:
  3.4 4.5 collective-permute-start.3
  14.2 4.9 collective-permute-done.1
  23.4 4.5 collective-permute-start.7
  36.6 4.5 collective-permute-start.11
  53.7 4.5 collective-permute-start.15
  65.2 4.8 collective-permute-start.19
  73.0 4.8 collective-permute-start.23
  87.0 4.6 collective-permute-start.27
  108.7 5.1 collective-permute-start.30
  115.2 5.6 collective-permute-done.31
  122.9 73.3 %while.84 = (s32[]{:T(128)}, f32[81,2048]{1,0:T(8,128)S(1)}, f32[8,3,27,128]{2,1,3,0:T(4,128)}, f32[8,128]{1,0:T(8,128)S(1)}, s32[8,128]{1,0:T(8,128)S(1)}, /*index=5*/f32[81,2048]{1,0:T(8,128)S(1)}, s32[]{:T(128)}, s32[]{:T(128)}) while((s32[]{:T(128)}, f32[81,2048]{1,0:T(8,128)S(1)}, f32[8,3,27,128]{2,1,3,0:T(4,128)}, ...), condition=%wide.region_13.14_spmd.clone, body=%wide.region_12.13_spmd.clone.sunk | while | flops 511215744 | bytes 3045039 | solution.py:167
  196.6 3.9 scatter-add.209
  200.5 3.9 scatter-add.210
  205.2 3.9 scatter-add.214
  211.0 5.7 scatter-add.215
  217.6 3.9 scatter-add.219
  221.6 3.9 scatter-add.220
  225.6 3.9 scatter-add.224
  234.3 3.9 scatter-add.229
  238.3 3.9 scatter-add.230
  242.9 3.9 scatter-add.234
  246.9 4.1 scatter-add.235
  251.2 3.9 scatter-add.239
  259.8 3.9 scatter-add.244
  263.8 3.9 scatter-add.245
  268.5 3.9 scatter-add.249
  272.5 3.9 scatter-add.250
  276.4 4.1 collective-permute-start.32
  282.6 4.6 collective-permute-done.33
  287.2 4.8 collective-permute-start.34
  293.5 4.1 collective-permute-done.35
  298.4 19.5 %all-reduce.51 = (f32[]{:T(128)}, f32[]{:T(128)}) all-reduce(f32[]{:T(128)} %get-tuple-element.879, f32[]{:T(128)} %get-tuple-element.878), channel_id=1, replica_groups=mesh['gx_0'=4,'gx_1'=4,'gx_2'=2,'gy'=16] {'gx_0'}, use_global_device_ids=true, to_apply=%region_8.9 | all-reduce | flops 2 | bytes 16 | tf_op jit(solution)/shard_map/psum | solution.py:54
  317.9 16.4 %all-reduce.49 = (f32[]{:T(128)}, f32[]{:T(128)}) all-reduce(f32[]{:T(128)} %get-tuple-element.914, f32[]{:T(128)} %get-tuple-element.915), channel_id=1, replica_groups=mesh['gx_0'=4,'gx_1'=4,'gx_2'=2,'gy'=16] {'gx_1'}, use_global_device_ids=true, to_apply=%region_9.10 | all-reduce | flops 2 | bytes 16 | tf_op jit(solution)/shard_map/psum | solution.py:54
  337.4 34.9 %all-reduce.47 = (f32[]{:T(128)}, f32[]{:T(128)}) all-reduce(f32[]{:T(128)} %get-tuple-element.918, f32[]{:T(128)} %get-tuple-element.919), channel_id=1, replica_groups=mesh['gx_0'=4,'gx_1'=4,'gx_2'=2,'gy'=16] {'gy'}, use_global_device_ids=true, to_apply=%region_11.12 | all-reduce | flops 2 | bytes 16 | tf_op jit(solution)/shard_map/psum | solution.py:54
  375.0 4.5 collective-permute-start.39
  389.8 4.5 collective-permute-start.43
  407.3 4.5 collective-permute-start.47
  418.8 4.8 collective-permute-start.51
  430.7 4.8 collective-permute-start.55
  438.4 4.8 collective-permute-start.59
  452.4 4.6 collective-permute-start.63
  471.1 4.8 collective-permute-start.66
  477.2 5.4 collective-permute-done.67
  484.7 73.5 %while.85 = (s32[]{:T(128)}, f32[81,2048]{1,0:T(8,128)S(1)}, f32[8,3,27,128]{2,1,3,0:T(4,128)}, f32[8,128]{1,0:T(8,128)S(1)}, s32[8,128]{1,0:T(8,128)S(1)}, /*index=5*/f32[81,2048]{1,0:T(8,128)S(1)}, s32[]{:T(128)}, s32[]{:T(128)}) while((s32[]{:T(128)}, f32[81,2048]{1,0:T(8,128)S(1)}, f32[8,3,27,128]{2,1,3,0:T(4,128)}, ...), condition=%wide.region_28.29_spmd.clone, body=%wide.region_27.28_spmd.clone.sunk | while | flops 511215744 | bytes 3045039 | solution.py:167
  558.6 3.9 scatter-add.260
  562.5 3.9 scatter-add.261
  567.2 3.9 scatter-add.265
  573.1 5.7 scatter-add.266
  579.7 3.9 scatter-add.270
  583.6 3.9 scatter-add.271
  596.3 3.9 scatter-add.280
  600.3 3.9 scatter-add.281
  605.0 3.9 scatter-add.285
  609.0 4.0 scatter-add.286
  621.9 3.9 scatter-add.295
  625.9 3.9 scatter-add.296
  630.5 3.9 scatter-add.300
  634.5 3.9 scatter-add.301
  644.2 4.0 collective-permute-done.69
  648.3 4.8 collective-permute-start.70
  654.5 4.1 collective-permute-done.71
  659.4 16.4 %all-reduce.50 = (f32[]{:T(128)}, f32[]{:T(128)}) all-reduce(f32[]{:T(128)} %get-tuple-element.877, f32[]{:T(128)} %get-tuple-element.876), channel_id=1, replica_groups=mesh['gx_0'=4,'gx_1'=4,'gx_2'=2,'gy'=16] {'gx_0'}, use_global_device_ids=true, to_apply=%region_23.24 | all-reduce | flops 2 | bytes 16 | tf_op jit(solution)/shard_map/psum | solution.py:54
  675.9 16.4 %all-reduce.48 = (f32[]{:T(128)}, f32[]{:T(128)}) all-reduce(f32[]{:T(128)} %get-tuple-element.912, f32[]{:T(128)} %get-tuple-element.913), channel_id=1, replica_groups=mesh['gx_0'=4,'gx_1'=4,'gx_2'=2,'gy'=16] {'gx_1'}, use_global_device_ids=true, to_apply=%region_24.25 | all-reduce | flops 2 | bytes 16 | tf_op jit(solution)/shard_map/psum | solution.py:54
  695.4 31.8 %all-reduce.46 = (f32[]{:T(128)}, f32[]{:T(128)}) all-reduce(f32[]{:T(128)} %get-tuple-element.916, f32[]{:T(128)} %get-tuple-element.917), channel_id=1, replica_groups=mesh['gx_0'=4,'gx_1'=4,'gx_2'=2,'gy'=16] {'gy'}, use_global_device_ids=true, to_apply=%region_26.27 | all-reduce | flops 2 | bytes 16 | tf_op jit(solution)/shard_map/psum | solution.py:54
  (761 shorter events, 344.1 us)
Async XLA Ops:
  2.1 12.0 %collective-permute-start.2 = (f32[3,4,1,128]{3,1,2,0:T(4,128)S(1)}, f32[3,4,1,128]{3,1,2,0:T(4,128)S(1)}, u32[]{:S(2)}, u32[]{:S(2)}) collective-permute-start(f32[3,4,1,128]{3,1,2,0:T(4,128)S(1)} %bitcast.243), channel_id=1, source_target_pairs={{1,0},{2,1},{3,2},{4,3},{5,4},{6,5},{7,6},{8,7},{9,8},{10,9},{11,1... | collective-permute-start | bytes 18440 | tf_op jit(solution)/shard_map/ppermute | solution.py:29
  3.4 10.7 %collective-permute-start.3 = (f32[3,4,1,128]{3,1,2,0:T(4,128)S(1)}, f32[3,4,1,128]{3,1,2,0:T(4,128)S(1)}, u32[]{:S(2)}, u32[]{:S(2)}) collective-permute-start(f32[3,4,1,128]{3,1,2,0:T(4,128)S(1)} %bitcast.241), channel_id=1, source_target_pairs={{0,1},{1,2},{2,3},{3,4},{4,5},{5,6},{6,7},{7,8},{8,9},{9,10},{10,1... | collective-permute-start | bytes 18440 | tf_op jit(solution)/shard_map/ppermute | solution.py:28
  8.0 6.2 collective-permute-start
  9.9 9.2 %collective-permute-start.1 = (f32[3,1,4,128]{3,2,1,0:T(4,128)S(1)}, f32[3,1,4,128]{3,2,1,0:T(4,128)S(1)}, u32[]{:S(2)}, u32[]{:S(2)}) collective-permute-start(f32[3,1,4,128]{3,2,1,0:T(4,128)S(1)} %get-tuple-element.1066), channel_id=1, source_target_pairs={{0,16},{16,32},{32,48},{48,64},{64,80},{80,96},{96,112},{112,128},... | collective-permute-start | bytes 18440 | tf_op jit(solution)/shard_map/ppermute | solution.py:28
  22.0 10.3 %collective-permute-start.6 = (f32[3,2,1,64]{3,2,1,0:T(1,128)S(1)}, f32[3,2,1,64]{3,2,1,0:T(1,128)S(1)}, u32[]{:S(2)}, u32[]{:S(2)}) collective-permute-start(f32[3,2,1,64]{3,2,1,0:T(1,128)S(1)} %get-tuple-element.1087), channel_id=1, source_target_pairs={{1,0},{2,1},{3,2},{4,3},{5,4},{6,5},{7,6},{8,7},{9,8},{10,9},{11,1... | collective-permute-start | bytes 4616 | tf_op jit(solution)/shard_map/ppermute | solution.py:29
  23.4 8.9 %collective-permute-start.7 = (f32[3,2,1,64]{3,2,1,0:T(1,128)S(1)}, f32[3,2,1,64]{3,2,1,0:T(1,128)S(1)}, u32[]{:S(2)}, u32[]{:S(2)}) collective-permute-start(f32[3,2,1,64]{3,2,1,0:T(1,128)S(1)} %get-tuple-element.1086), channel_id=1, source_target_pairs={{0,1},{1,2},{2,3},{3,4},{4,5},{5,6},{6,7},{7,8},{8,9},{9,10},{10,1... | collective-permute-start | bytes 4616 | tf_op jit(solution)/shard_map/ppermute | solution.py:28
  29.9 4.9 collective-permute-start.5
  35.3 10.2 %collective-permute-start.10 = (f32[3,1,1,32]{3,0,2,1:T(4,128)S(1)}, f32[3,1,1,32]{3,0,2,1:T(4,128)S(1)}, u32[]{:S(2)}, u32[]{:S(2)}) collective-permute-start(f32[3,1,1,32]{3,0,2,1:T(4,128)S(1)} %fusion.144), channel_id=1, source_target_pairs={{1,0},{2,1},{3,2},{4,3},{5,4},{6,5},{7,6},{8,7},{9,8},{10,9},{11,1... | collective-permute-start | bytes 1160 | tf_op jit(solution)/shard_map/ppermute | solution.py:29
  36.6 8.9 %collective-permute-start.11 = (f32[3,1,1,32]{3,0,2,1:T(4,128)S(1)}, f32[3,1,1,32]{3,0,2,1:T(4,128)S(1)}, u32[]{:S(2)}, u32[]{:S(2)}) collective-permute-start(f32[3,1,1,32]{3,0,2,1:T(4,128)S(1)} %fusion.144), channel_id=1, source_target_pairs={{0,1},{1,2},{2,3},{3,4},{4,5},{5,6},{6,7},{7,8},{8,9},{9,10},{10,1... | collective-permute-start | bytes 1160 | tf_op jit(solution)/shard_map/ppermute | solution.py:28
  43.0 4.9 collective-permute-start.9
  48.0 10.2 %collective-permute-start.12 = (f32[3,1,1,32]{3,0,2,1:T(4,128)S(1)}, f32[3,1,1,32]{3,0,2,1:T(4,128)S(1)}, u32[]{:S(2)}, u32[]{:S(2)}) collective-permute-start(f32[3,1,1,32]{3,0,2,1:T(4,128)S(1)} %divide_add_fusion.9), channel_id=1, source_target_pairs={{16,0},{32,16},{48,32},{64,48},{80,64},{96,80},{112,96},{128,112},... | collective-permute-start | bytes 1160 | tf_op jit(solution)/shard_map/ppermute | solution.py:29
  50.0 8.3 %collective-permute-start.13 = (f32[3,1,1,32]{3,0,2,1:T(4,128)S(1)}, f32[3,1,1,32]{3,0,2,1:T(4,128)S(1)}, u32[]{:S(2)}, u32[]{:S(2)}) collective-permute-start(f32[3,1,1,32]{3,0,2,1:T(4,128)S(1)} %divide_add_fusion.9), channel_id=1, source_target_pairs={{0,16},{16,32},{32,48},{48,64},{64,80},{80,96},{96,112},{112,128},... | collective-permute-start | bytes 1160 | tf_op jit(solution)/shard_map/ppermute | solution.py:28
  52.4 5.9 collective-permute-start.14
  53.7 5.8 collective-permute-start.15
  59.6 10.5 %collective-permute-start.16 = (f32[3,1,1,32]{3,0,2,1:T(4,128)S(1)}, f32[3,1,1,32]{3,0,2,1:T(4,128)S(1)}, u32[]{:S(2)}, u32[]{:S(2)}) collective-permute-start(f32[3,1,1,32]{3,0,2,1:T(4,128)S(1)} %divide_add_fusion.8), channel_id=1, source_target_pairs={{16,0},{32,16},{48,32},{64,48},{80,64},{96,80},{112,96},{128,112},... | collective-permute-start | bytes 1160 | tf_op jit(solution)/shard_map/ppermute | solution.py:29
  61.6 8.4 %collective-permute-start.17 = (f32[3,1,1,32]{3,0,2,1:T(4,128)S(1)}, f32[3,1,1,32]{3,0,2,1:T(4,128)S(1)}, u32[]{:S(2)}, u32[]{:S(2)}) collective-permute-start(f32[3,1,1,32]{3,0,2,1:T(4,128)S(1)} %divide_add_fusion.8), channel_id=1, source_target_pairs={{0,16},{16,32},{32,48},{48,64},{64,80},{80,96},{96,112},{112,128},... | collective-permute-start | bytes 1160 | tf_op jit(solution)/shard_map/ppermute | solution.py:28
  63.9 6.1 collective-permute-start.18
  65.2 6.1 collective-permute-start.19
  71.7 10.5 %collective-permute-start.22 = (f32[3,2,1,64]{3,2,1,0:T(1,128)S(1)}, f32[3,2,1,64]{3,2,1,0:T(1,128)S(1)}, u32[]{:S(2)}, u32[]{:S(2)}) collective-permute-start(f32[3,2,1,64]{3,2,1,0:T(1,128)S(1)} %get-tuple-element.1083), channel_id=1, source_target_pairs={{1,0},{2,1},{3,2},{4,3},{5,4},{6,5},{7,6},{8,7},{9,8},{10,9},{11,1... | collective-permute-start | bytes 4616 | tf_op jit(solution)/shard_map/ppermute | solution.py:29
  73.0 9.2 %collective-permute-start.23 = (f32[3,2,1,64]{3,2,1,0:T(1,128)S(1)}, f32[3,2,1,64]{3,2,1,0:T(1,128)S(1)}, u32[]{:S(2)}, u32[]{:S(2)}) collective-permute-start(f32[3,2,1,64]{3,2,1,0:T(1,128)S(1)} %get-tuple-element.1082), channel_id=1, source_target_pairs={{0,1},{1,2},{2,3},{3,4},{4,5},{5,6},{6,7},{7,8},{8,9},{9,10},{10,1... | collective-permute-start | bytes 4616 | tf_op jit(solution)/shard_map/ppermute | solution.py:28
  79.7 4.9 collective-permute-start.21
  85.7 10.2 %collective-permute-start.26 = (f32[3,4,1,128]{3,1,2,0:T(4,128)S(1)}, f32[3,4,1,128]{3,1,2,0:T(4,128)S(1)}, u32[]{:S(2)}, u32[]{:S(2)}) collective-permute-start(f32[3,4,1,128]{3,1,2,0:T(4,128)S(1)} %bitcast.248), channel_id=1, source_target_pairs={{1,0},{2,1},{3,2},{4,3},{5,4},{6,5},{7,6},{8,7},{9,8},{10,9},{11,1... | collective-permute-start | bytes 18440 | tf_op jit(solution)/shard_map/ppermute | solution.py:29
  87.0 9.0 %collective-permute-start.27 = (f32[3,4,1,128]{3,1,2,0:T(4,128)S(1)}, f32[3,4,1,128]{3,1,2,0:T(4,128)S(1)}, u32[]{:S(2)}, u32[]{:S(2)}) collective-permute-start(f32[3,4,1,128]{3,1,2,0:T(4,128)S(1)} %bitcast.245), channel_id=1, source_target_pairs={{0,1},{1,2},{2,3},{3,4},{4,5},{5,6},{6,7},{7,8},{8,9},{9,10},{10,1... | collective-permute-start | bytes 18440 | tf_op jit(solution)/shard_map/ppermute | solution.py:28
  93.5 4.9 collective-permute-start.25
  98.7 8.3 %collective-permute-start.28 = (f32[3,1,4,128]{3,2,1,0:T(4,128)S(1)}, f32[3,1,4,128]{3,2,1,0:T(4,128)S(1)}, u32[]{:S(2)}, u32[]{:S(2)}) collective-permute-start(f32[3,1,4,128]{3,2,1,0:T(4,128)S(1)} %get-tuple-element.1060), channel_id=1, source_target_pairs={{0,16},{16,32},{32,48},{48,64},{64,80},{80,96},{96,112},{112,128},... | collective-permute-start | bytes 18440 | tf_op jit(solution)/shard_map/ppermute | solution.py:47
  102.0 6.6 collective-permute-start.29
  108.7 6.5 collective-permute-start.30
  113.8 7.0 collective-permute-start.31
  276.4 6.1 collective-permute-start.32
  280.6 6.6 collective-permute-start.33
  287.2 6.2 collective-permute-start.34
  292.1 5.5 collective-permute-start.35
  373.7 10.2 %collective-permute-start.38 = (f32[3,4,1,128]{3,1,2,0:T(4,128)S(1)}, f32[3,4,1,128]{3,1,2,0:T(4,128)S(1)}, u32[]{:S(2)}, u32[]{:S(2)}) collective-permute-start(f32[3,4,1,128]{3,1,2,0:T(4,128)S(1)} %bitcast.249), channel_id=1, source_target_pairs={{1,0},{2,1},{3,2},{4,3},{5,4},{6,5},{7,6},{8,7},{9,8},{10,9},{11,1... | collective-permute-start | bytes 18440 | tf_op jit(solution)/shard_map/ppermute | solution.py:29
  375.0 8.9 %collective-permute-start.39 = (f32[3,4,1,128]{3,1,2,0:T(4,128)S(1)}, f32[3,4,1,128]{3,1,2,0:T(4,128)S(1)}, u32[]{:S(2)}, u32[]{:S(2)}) collective-permute-start(f32[3,4,1,128]{3,1,2,0:T(4,128)S(1)} %bitcast.246), channel_id=1, source_target_pairs={{0,1},{1,2},{2,3},{3,4},{4,5},{5,6},{6,7},{7,8},{8,9},{9,10},{10,1... | collective-permute-start | bytes 18440 | tf_op jit(solution)/shard_map/ppermute | solution.py:28
  381.5 4.9 collective-permute-start.37
  388.5 10.2 %collective-permute-start.42 = (f32[3,2,1,64]{3,2,1,0:T(1,128)S(1)}, f32[3,2,1,64]{3,2,1,0:T(1,128)S(1)}, u32[]{:S(2)}, u32[]{:S(2)}) collective-permute-start(f32[3,2,1,64]{3,2,1,0:T(1,128)S(1)} %get-tuple-element.1079), channel_id=1, source_target_pairs={{1,0},{2,1},{3,2},{4,3},{5,4},{6,5},{7,6},{8,7},{9,8},{10,9},{11,1... | collective-permute-start | bytes 4616 | tf_op jit(solution)/shard_map/ppermute | solution.py:29
  389.8 8.9 %collective-permute-start.43 = (f32[3,2,1,64]{3,2,1,0:T(1,128)S(1)}, f32[3,2,1,64]{3,2,1,0:T(1,128)S(1)}, u32[]{:S(2)}, u32[]{:S(2)}) collective-permute-start(f32[3,2,1,64]{3,2,1,0:T(1,128)S(1)} %get-tuple-element.1078), channel_id=1, source_target_pairs={{0,1},{1,2},{2,3},{3,4},{4,5},{5,6},{6,7},{7,8},{8,9},{9,10},{10,1... | collective-permute-start | bytes 4616 | tf_op jit(solution)/shard_map/ppermute | solution.py:28
  396.3 4.9 collective-permute-start.41
  401.6 10.2 %collective-permute-start.44 = (f32[3,1,1,32]{3,0,2,1:T(4,128)S(1)}, f32[3,1,1,32]{3,0,2,1:T(4,128)S(1)}, u32[]{:S(2)}, u32[]{:S(2)}) collective-permute-start(f32[3,1,1,32]{3,0,2,1:T(4,128)S(1)} %fusion.140), channel_id=1, source_target_pairs={{16,0},{32,16},{48,32},{64,48},{80,64},{96,80},{112,96},{128,112},... | collective-permute-start | bytes 1160 | tf_op jit(solution)/shard_map/ppermute | solution.py:29
  403.5 8.3 %collective-permute-start.45 = (f32[3,1,1,32]{3,0,2,1:T(4,128)S(1)}, f32[3,1,1,32]{3,0,2,1:T(4,128)S(1)}, u32[]{:S(2)}, u32[]{:S(2)}) collective-permute-start(f32[3,1,1,32]{3,0,2,1:T(4,128)S(1)} %fusion.140), channel_id=1, source_target_pairs={{0,16},{16,32},{32,48},{48,64},{64,80},{80,96},{96,112},{112,128},... | collective-permute-start | bytes 1160 | tf_op jit(solution)/shard_map/ppermute | solution.py:28
  406.0 5.9 collective-permute-start.46
  407.3 5.8 collective-permute-start.47
  413.2 10.5 %collective-permute-start.48 = (f32[3,1,1,32]{3,0,2,1:T(4,128)S(1)}, f32[3,1,1,32]{3,0,2,1:T(4,128)S(1)}, u32[]{:S(2)}, u32[]{:S(2)}) collective-permute-start(f32[3,1,1,32]{3,0,2,1:T(4,128)S(1)} %divide_add_fusion.6), channel_id=1, source_target_pairs={{16,0},{32,16},{48,32},{64,48},{80,64},{96,80},{112,96},{128,112},... | collective-permute-start | bytes 1160 | tf_op jit(solution)/shard_map/ppermute | solution.py:29
  415.2 8.4 %collective-permute-start.49 = (f32[3,1,1,32]{3,0,2,1:T(4,128)S(1)}, f32[3,1,1,32]{3,0,2,1:T(4,128)S(1)}, u32[]{:S(2)}, u32[]{:S(2)}) collective-permute-start(f32[3,1,1,32]{3,0,2,1:T(4,128)S(1)} %divide_add_fusion.6), channel_id=1, source_target_pairs={{0,16},{16,32},{32,48},{48,64},{64,80},{80,96},{96,112},{112,128},... | collective-permute-start | bytes 1160 | tf_op jit(solution)/shard_map/ppermute | solution.py:28
  417.5 6.1 collective-permute-start.50
  418.8 6.1 collective-permute-start.51
  425.0 10.5 %collective-permute-start.52 = (f32[3,1,1,32]{3,0,2,1:T(4,128)S(1)}, f32[3,1,1,32]{3,0,2,1:T(4,128)S(1)}, u32[]{:S(2)}, u32[]{:S(2)}) collective-permute-start(f32[3,1,1,32]{3,0,2,1:T(4,128)S(1)} %divide_add_fusion.5), channel_id=1, source_target_pairs={{16,0},{32,16},{48,32},{64,48},{80,64},{96,80},{112,96},{128,112},... | collective-permute-start | bytes 1160 | tf_op jit(solution)/shard_map/ppermute | solution.py:29
  427.3 8.2 %collective-permute-start.53 = (f32[3,1,1,32]{3,0,2,1:T(4,128)S(1)}, f32[3,1,1,32]{3,0,2,1:T(4,128)S(1)}, u32[]{:S(2)}, u32[]{:S(2)}) collective-permute-start(f32[3,1,1,32]{3,0,2,1:T(4,128)S(1)} %divide_add_fusion.5), channel_id=1, source_target_pairs={{0,16},{16,32},{32,48},{48,64},{64,80},{80,96},{96,112},{112,128},... | collective-permute-start | bytes 1160 | tf_op jit(solution)/shard_map/ppermute | solution.py:28
  429.4 6.1 collective-permute-start.54
  430.7 6.1 collective-permute-start.55
  437.1 10.5 %collective-permute-start.58 = (f32[3,2,1,64]{3,2,1,0:T(1,128)S(1)}, f32[3,2,1,64]{3,2,1,0:T(1,128)S(1)}, u32[]{:S(2)}, u32[]{:S(2)}) collective-permute-start(f32[3,2,1,64]{3,2,1,0:T(1,128)S(1)} %get-tuple-element.1075), channel_id=1, source_target_pairs={{1,0},{2,1},{3,2},{4,3},{5,4},{6,5},{7,6},{8,7},{9,8},{10,9},{11,1... | collective-permute-start | bytes 4616 | tf_op jit(solution)/shard_map/ppermute | solution.py:29
  438.4 9.2 %collective-permute-start.59 = (f32[3,2,1,64]{3,2,1,0:T(1,128)S(1)}, f32[3,2,1,64]{3,2,1,0:T(1,128)S(1)}, u32[]{:S(2)}, u32[]{:S(2)}) collective-permute-start(f32[3,2,1,64]{3,2,1,0:T(1,128)S(1)} %get-tuple-element.1074), channel_id=1, source_target_pairs={{0,1},{1,2},{2,3},{3,4},{4,5},{5,6},{6,7},{7,8},{8,9},{9,10},{10,1... | collective-permute-start | bytes 4616 | tf_op jit(solution)/shard_map/ppermute | solution.py:28
  445.1 4.9 collective-permute-start.57
  451.1 10.2 %collective-permute-start.62 = (f32[3,4,1,128]{3,1,2,0:T(4,128)S(1)}, f32[3,4,1,128]{3,1,2,0:T(4,128)S(1)}, u32[]{:S(2)}, u32[]{:S(2)}) collective-permute-start(f32[3,4,1,128]{3,1,2,0:T(4,128)S(1)} %bitcast.250), channel_id=1, source_target_pairs={{1,0},{2,1},{3,2},{4,3},{5,4},{6,5},{7,6},{8,7},{9,8},{10,9},{11,1... | collective-permute-start | bytes 18440 | tf_op jit(solution)/shard_map/ppermute | solution.py:29
  452.4 8.9 %collective-permute-start.63 = (f32[3,4,1,128]{3,1,2,0:T(4,128)S(1)}, f32[3,4,1,128]{3,1,2,0:T(4,128)S(1)}, u32[]{:S(2)}, u32[]{:S(2)}) collective-permute-start(f32[3,4,1,128]{3,1,2,0:T(4,128)S(1)} %bitcast.247), channel_id=1, source_target_pairs={{0,1},{1,2},{2,3},{3,4},{4,5},{5,6},{6,7},{7,8},{8,9},{9,10},{10,1... | collective-permute-start | bytes 18440 | tf_op jit(solution)/shard_map/ppermute | solution.py:28
  458.9 4.9 collective-permute-start.61
  464.1 5.6 collective-permute-start.64
  466.1 5.0 collective-permute-start.65
  471.1 6.1 collective-permute-start.66
  475.8 6.8 collective-permute-start.67
  638.5 5.6 collective-permute-start.68
  641.6 6.6 collective-permute-start.69
  648.3 6.2 collective-permute-start.70
  653.1 5.5 collective-permute-start.71
  (14 other events, 469.4 us)
where the time goes:
time: 742 us; the launch traced here: 733 us
  starting transfers between devices  191 us (26%)
  local copies, waits for them, and re-layouts  188 us (25%)
  blocking collectives  142 us (19%)
  matrix products  90.9 us (12%)
  waiting for transfers between devices  61.8 us (8%)
  other arithmetic  47.7 us (6%)
  between operations  9.82 us (1%)
    scatter-add x50, local copies, waits for them, and re-layouts, stiffness_local(): spread = spread.at[:, off_a:off_a + rows_x, off_b:off_b + rows_y, off_c:o...  151 us
    psum x8, blocking collectives, over_axes(): return functools.reduce(lax.psum, axes, array)  142 us
    ppermute x28, starting transfers between devices, extended(): lax.ppermute(last, axis, up)  98 us
    ppermute x28, starting transfers between devices, extended(): lax.ppermute(leading, axis, [(b, a) for a, b in up])  45.7 us
    dot_general x16, matrix products, particle_forces(): jnp.einsum('...ijp,...jnp->...inp', stress, gradients, precision=lax.Prec...  33.5 us
    mul x16, other arithmetic, particle_forces(): stress = stress + identity * (first_lame * strain_trace)[..., None, None, :]  32.2 us
    ppermute x8, starting transfers between devices, padded_2(): before = lax.ppermute(last, axis, up)  31.9 us
    dot_general x16, matrix products, particle_forces(): jnp.einsum('...inp,...jnp->...ijp', values, gradients, precision=lax.Prec...  30.9 us
  transfers between devices with their start and end apart: 72, of which 22 were waited for; matrix products, arithmetic and copies ran while one was open for 1% of the time, Pallas kernels for 0%

commit v1 on v0

v1 whole, which is shorter than its diff:
```python
import jax
import jax.numpy as jnp
from jax import lax
from jax.experimental import pallas as pl
from jax.experimental.pallas import tpu as pltpu
from jax.sharding import PartitionSpec as P

MESH = pl.DeviceIdType.MESH
F32 = jnp.float32
BF16 = jnp.bfloat16
LANES = 128
POISSON = 0.3
NEAR = tuple(
    (dx, dy)
    for dx, dy in ((0, 1), (0, -1), (1, 1), (1, -1), (-1, 1), (-1, -1), (1, 0), (-1, 0))
)
FAR = tuple(
    sorted(
        (
            (dx, dy)
            for dx in range(-4, 5)
            for dy in range(-4, 5)
            if (dx, dy) != (0, 0) and max(abs(dx) - 1, 0) + max(abs(dy) - 1, 0) <= 3
        ),
        key=lambda d: -abs(d[0]) - abs(d[1]),
    )
)
ROWS = 112


def first_cut(d, diagonal):
    if d == 0:
        return (0, 4)
    wide = 2 if diagonal else 3
    return (4 - wide, 4) if d > 0 else (0, wide)


def first_place(d, diagonal):
    if d == 0:
        return (3, 7)
    wide = 2 if diagonal else 3
    return (7, 7 + wide) if d > 0 else (3 - wide, 3)


def wide_cut(d, diagonal):
    return ((0, 4), (0, 6), (2, 6))[d + 1]


def wide_place(d, diagonal):
    return ((0, 4), (2, 8), (6, 10))[d + 1]


def thin_cut(d, diagonal):
    return ((0, 1), (1, 5), (5, 6))[d + 1]


def thin_place(d, diagonal):
    return ((0, 1), (0, 4), (3, 4))[d + 1]


def box(cut, d):
    diagonal = d[0] != 0 and d[1] != 0
    (x0, x1), (y0, y1) = cut(d[0], diagonal), cut(d[1], diagonal)
    return slice(x0, x1), slice(y0, y1)


def extent(cut, d, rows):
    sx, sy = box(cut, d)
    return (sx.stop - sx.start, sy.stop - sy.start, rows, LANES)


def kernel(n_gx, n_gy, *refs):
    (b_hbm, m_hbm, g_hbm, s_hbm, v_hbm, n_hbm, x_ref, r_ref), refs = refs[:8], refs[8:]
    first_in, wide_in, thin_in = refs[:8], refs[8:16], refs[16:24]
    one_in = (refs[24:32], refs[32:40])
    (b_in, m_in, g_in, s_in, v_in, n_in), refs = refs[40:46], refs[46:]
    (
        grad, own, rhs0, rhs1, mass, inv0, e0_ref, one_own0, one_own1, one_rhs, one_inv,
        far_own0, far_own1, far_in0, far_in1, far_rhs, far_inv, far_est, z_ref, u_ref,
        z_shift, f_rows, lhs_hi, lhs_lo, hot, rows_out, part0, part1, sums, sum_own,
        sum_own2, line_in, line_in2, near_send, near_recv, far_send, far_recv,
        line_send, line_recv, local_sem,
    ) = refs

    gx, gy = lax.axis_index("gx"), lax.axis_index("gy")

    def device(dx, dy):
        return {"gx": lax.rem(gx + (dx % n_gx), n_gx), "gy": lax.rem(gy + (dy % n_gy), n_gy)}

    loads = [
        pltpu.make_async_copy(src, dst, local_sem.at[i])
        for i, (src, dst) in enumerate(
            (
                (b_hbm, b_in), (m_hbm, m_in), (g_hbm.at[0, 0], g_in),
                (s_hbm.at[0, 0], s_in), (v_hbm.at[0, 0], v_in), (n_hbm.at[0, 0], n_in),
            )
        )
    ]
    for load in loads:
        load.start()
    partners = {(dx % n_gx, dy % n_gy) for dx, dy in FAR}
    partners |= {(d, 0) for d in range(1, n_gx)} | {(0, d) for d in range(1, n_gy)}
    partners = sorted(partners)
    barrier = pltpu.get_barrier_semaphore()
    for dx, dy in partners:
        pl.semaphore_signal(barrier, inc=1, device_id=device(dx, dy), device_id_type=MESH)
    for load in (loads[0], loads[1]):
        load.wait()
    for x in range(4):
        for y in range(4):
            for m in range(3):
                own[x, y, m : m + 1, :] = b_in[m, x, y : y + 1, :]
            own[x, y, 3:4, :] = m_in[x, y : y + 1, :]
    rhs0[3:7, 3:7] = own[:, :, 0:3, :]
    mass[3:7, 3:7] = own[:, :, 3:4, :]

    pl.semaphore_wait(barrier, len(partners))

    started = []

    def send(src, dst, group, i, d):
        copy = pltpu.make_async_remote_copy(
            src_ref=src,
            dst_ref=dst,
            send_sem=near_send.at[group, i],
            recv_sem=near_recv.at[group, NEAR.index((-d[0], -d[1]))],
            device_id=device(*d),
            device_id_type=MESH,
        )
        copy.start()
        started.append(copy)

    def arrived(dst, group, i):
        pltpu.make_async_copy(dst, dst, near_recv.at[group, i]).wait()

    def other(d):
        return NEAR.index((-d[0], -d[1]))

    for i, d in enumerate(NEAR):
        sx, sy = box(lambda *a: first_cut(*a), d)
        send(own.at[sx, sy], first_in[other(d)], 0, i, d)

    lane4 = lax.broadcasted_iota(jnp.int32, (1, 1, 3, LANES), 3)

    def ones_where(cond):
        return jnp.where(cond, 1.0, 0.0).astype(F32)

    low_ok = {s: ones_where(lane4 >= s) for s in (1, 2, 4)}
    high_ok = {s: ones_where(lane4 < LANES - s) for s in (1, 2, 4)}
    odd = {s: ones_where((lane4 & s) != 0) for s in (1, 2)}
    even = {s: ones_where((lane4 & s) == 0) for s in (1, 2)}

    def turn(v, s):
        return pltpu.roll(v, s % LANES, v.ndim - 1)

    def beside_z(v, s):
        return turn(v, s) * low_ok[s] + turn(v, -s) * high_ok[s]

    def pair_z(v, s):
        return v + turn(v, s) * odd[s] + turn(v, -s) * even[s]

    def coarser(v, s):
        nx, ny = v.shape[0] // 2, v.shape[1] // 2
        w = v.reshape((nx, 2, ny, 2) + v.shape[2:])
        w = (w[:, 0] + w[:, 1])
        w = w[:, :, 0] + w[:, :, 1]
        return pair_z(w, s)

    def finer(v):
        nx, ny = v.shape[:2]
        w = jnp.broadcast_to(v[:, None, :, None], (nx, 2, ny, 2) + v.shape[2:])
        return w.reshape((2 * nx, 2 * ny) + v.shape[2:])

    lane2 = lax.broadcasted_iota(jnp.int32, (8, LANES), 1)
    sub2 = lax.broadcasted_iota(jnp.int32, (8, LANES), 0)
    pack_mask = ones_where((lane2 & 3) == sub2)[0:3]
    mass_mask = ones_where((lane2 & 3) == 3)[0:1]
    unpack_index = (lane2 & ~3) + jnp.minimum(sub2, 2)
    inside = (
        (ones_where(gx > 0), ones_where(gx < n_gx - 1)),
        (ones_where(gy > 0), ones_where(gy < n_gy - 1)),
    )

    for load in loads[2:]:
        load.wait()
    for t in range(81):
        grad[t] = g_in[:, t // 27, t % 27, :]
    node = n_in[...]
    quotient = (node * 2017) >> 18
    k_index = node - quotient * 130
    i_index = (quotient * 43) >> 8
    j_index = quotient - i_index * 6
    effective = s_in[...] * v_in[...].astype(F32)
    z_rows = lax.broadcasted_iota(jnp.int32, (LANES, LANES), 0)
    for s in range(8):
        same = jnp.broadcast_to(k_index[s : s + 1, :], (LANES, LANES)) == z_rows
        hot[:, s * LANES : (s + 1) * LANES] = ones_where(same).astype(BF16)
    shear = effective * (0.5 / (1.0 + POISSON))
    lame = effective * (POISSON / ((1.0 + POISSON) * (1.0 - 2.0 * POISSON)))

    def particles(field, part):
        v = field[...]
        z_shift[0] = turn(v, 1) * low_ok[1]
        z_shift[1] = v
        z_shift[2] = turn(v, -1) * high_ok[1]
        i_lo, i_hi = (i_index & 1) != 0, (i_index & 2) != 0
        j_lo, j_hi = (j_index & 1) != 0, (j_index & 2) != 0

        def four(v0, v1, v2, v3, lo, hi):
            return jnp.where(hi, jnp.where(lo, v3, v2), jnp.where(lo, v1, v0))

        def gather(c, disp):
            disp = list(disp)
            for m in range(3):
                picked = [
                    [
                        jnp.take_along_axis(
                            jnp.broadcast_to(z_shift[c, x, y, m : m + 1, :], (8, LANES)),
                            k_index,
                            axis=1,
                            mode="promise_in_bounds",
                        )
                        for y in range(6)
                    ]
                    for x in range(6)
                ]
                for a in range(3):
                    row = [
                        four(*(picked[a + i][y] for i in range(4)), i_lo, i_hi) for y in range(6)
                    ]
                    for b in range(3):
                        value = four(*row[b : b + 4], j_lo, j_hi)
                        for l in range(3):
                            at = grad[l * 27 + 9 * a + 3 * b + c]
                            disp[3 * m + l] = disp[3 * m + l] + value * at
            return tuple(disp)

        zero = jnp.zeros((8, LANES), F32)
        disp = lax.fori_loop(0, 3, gather, (zero,) * 9)
        trace = lame * (disp[0] + disp[4] + disp[8])
        stress = [
            shear * (disp[3 * m + l] + disp[3 * l + m]) + (trace if m == l else 0.0)
            for m in range(3)
            for l in range(3)
        ]
        energy = sum(stress[q] * disp[q] for q in range(9))

        def scatter(c, carry):
            for m in range(3):
                spread = []
                for a in range(3):
                    force = []
                    for b in range(3):
                        t = 9 * a + 3 * b + c
                        force.append(sum(stress[3 * m + l] * grad[l * 27 + t] for l in range(3)))
                    spread.append(
                        [
                            sum(
                                jnp.where(j_index == y - b, force[b], 0.0)
                                for b in range(3)
                                if 0 <= y - b <= 3
                            )
                            for y in range(6)
                        ]
                    )
                for x in range(6):
                    for y in range(6):
                        f_rows[c * ROWS + (x * 6 + y) * 3 + m] = sum(
                            jnp.where(i_index == x - a, spread[a][y], 0.0)
                            for a in range(3)
                            if 0 <= x - a <= 3
                        )
            return carry

        lax.fori_loop(0, 3, scatter, 0)
        for s in range(8):
            rows = f_rows[:, s, :]
            high = rows.astype(BF16)
            lhs_hi[:, s * LANES : (s + 1) * LANES] = high
            lhs_lo[:, s * LANES : (s + 1) * LANES] = (rows - high.astype(F32)).astype(BF16)
        contract = (((1,), (1,)), ((), ()))
        total = lax.dot_general(lhs_hi[...], hot[...], contract, preferred_element_type=F32)
        total = total + lax.dot_general(
            lhs_lo[...], hot[...], contract, preferred_element_type=F32
        )
        rows_out[...] = (
            turn(total[0:ROWS], -1) * high_ok[1][0, 0, 0:1]
            + total[ROWS : 2 * ROWS]
            + turn(total[2 * ROWS : 3 * ROWS], 1) * low_ok[1][0, 0, 0:1]
        )
        for n in range(36):
            part[n // 6, n % 6] = rows_out[3 * n : 3 * n + 3, :]
        part[1:5, 1:5] = part[1:5, 1:5] + mass[3:7, 3:7] * field[1:5, 1:5]
        return energy

    def multigrid(turn_no, rhs, field):
        one_own = (one_own0, one_own1)[turn_no]
        far_own = (far_own0, far_own1)[turn_no]
        far_slots = (far_in0, far_in1)[turn_no]
        e0_ref[...] = inv0[...] * rhs[...]
        r0 = (
            0.3 * rhs[1:9, 1:9]
            + e0_ref[0:8, 1:9]
            + e0_ref[2:10, 1:9]
            + e0_ref[1:9, 0:8]
            + e0_ref[1:9, 2:10]
            + beside_z(e0_ref[1:9, 1:9], 1)
        )
        b1 = coarser(r0, 1)
        one_own[:, :, 0:3, :] = b1[1:3, 1:3]
        if turn_no == 0:
            mass1 = coarser(jnp.broadcast_to(mass[1:9, 1:9], (8, 8, 3, LANES)), 1)
            inv1 = 0.7 / (mass1 + 12.0)
            one_own[:, :, 3:4, :] = mass1[1:3, 1:3, 0:1]
            one_inv[1:5, 1:5] = inv1
            one_inv[1:2, 1:5] = one_inv[1:2, 1:5] * inside[0][0]
            one_inv[4:5, 1:5] = one_inv[4:5, 1:5] * inside[0][1]
            one_inv[1:5, 1:2] = one_inv[1:5, 1:2] * inside[1][0]
            one_inv[1:5, 4:5] = one_inv[1:5, 4:5] * inside[1][1]
        else:
            one_own[:, :, 3:4, :] = one_own0[:, :, 3:4, :]
        for i, d in enumerate(NEAR):
            send(one_own, one_in[turn_no][other(d)], 1 + turn_no, i, d)
        e1 = one_inv[1:5, 1:5] * b1
        r1 = 0.3 * b1[1:3, 1:3] + 2.0 * (
            e1[0:2, 1:3] + e1[2:4, 1:3] + e1[1:3, 0:2] + e1[1:3, 2:4] + beside_z(e1[1:3, 1:3], 2)
        )
        b2 = coarser(r1, 2)[0, 0]
        packed = jnp.sum(b2 * pack_mask, axis=0, keepdims=True)
        if turn_no == 0:
            mass2 = coarser(mass1[1:3, 1:3], 2)[0, 0]
            packed = packed + mass2[0:1] * mass_mask
        far_own[...] = packed
        for dx, dy in FAR:
            copy = pltpu.make_async_remote_copy(
                src_ref=far_own,
                dst_ref=far_slots.at[(4 - dx) * 9 + 4 - dy],
                send_sem=far_send.at[turn_no],
                recv_sem=far_recv.at[turn_no],
                device_id=device(dx, dy),
                device_id_type=MESH,
            )
            copy.start()
        one_rhs[2:4, 2:4] = one_own[:, :, 0:3, :]
        for i, d in enumerate(NEAR):
            got = one_in[turn_no][i]
            arrived(got, 1 + turn_no, i)
            sx, sy = slice(2 + 2 * d[0], 4 + 2 * d[0]), slice(2 + 2 * d[1], 4 + 2 * d[1])
            one_rhs[sx, sy] = got[:, :, 0:3, :]
            if turn_no == 0:
                keep = jnp.float32(1.0)
                if d[0]:
                    keep = keep * inside[0][(d[0] + 1) // 2]
                if d[1]:
                    keep = keep * inside[1][(d[1] + 1) // 2]
                beside = jnp.broadcast_to(got[:, :, 3:4, :], (2, 2, 3, LANES))
                one_inv[sx, sy] = (0.7 / (beside + 12.0)) * keep
        far_all = far_slots.at[pl.ds(0, len(FAR))]
        pltpu.make_async_copy(far_all, far_all, far_recv.at[turn_no]).wait()
        for dx, dy in FAR:
            far_rhs[dx + 4, dy + 4 : dy + 5, :] = far_slots[(dx + 4) * 9 + dy + 4]
        far_rhs[4, 4:5, :] = far_own[...]
        b = far_rhs[...]
        if turn_no == 0:
            quarter = lax.broadcasted_iota(jnp.int32, b.shape, 2) & 3
            diagonal = jnp.where(
                quarter == 0, turn(b, -3), jnp.where(quarter == 1, turn(b, -2), turn(b, -1))
            )
            at_x = lax.broadcasted_iota(jnp.int32, b.shape, 0) + (gx - 4)
            at_y = lax.broadcasted_iota(jnp.int32, b.shape, 1) + (gy - 4)
            within = (at_x >= 0) & (at_x < n_gx) & (at_y >= 0) & (at_y < n_gy)
            far_inv[...] = jnp.where(within, 0.7 / (diagonal + 24.0), 0.0)
        est = far_inv[...] * b
        for sweep in range(3):
            lo, hi = sweep + 1, 8 - sweep
            mid = est[1:-1]
            near = est[:-2] + est[2:] + pltpu.roll(mid, 1, 1) + pltpu.roll(mid, 15, 1)
            near = near + turn(mid, 4) * low_ok[4][0, :, 0:1] + turn(mid, -4) * high_ok[4][0, :, 0:1]
            est = 0.3 * mid + far_inv[lo:hi] * (b[lo:hi] + 4.0 * near)
        far_est[...] = est
        b1 = one_rhs[...]
        inv1 = one_inv[...]
        e2 = jnp.stack(
            [
                jnp.stack(
                    [
                        jnp.take_along_axis(
                            jnp.broadcast_to(far_est[x, 3 + y : 4 + y, :], (8, LANES)),
                            unpack_index,
                            axis=1,
                            mode="promise_in_bounds",
                        )[0:3]
                        for y in range(3)
                    ]
                )
                for x in range(3)
            ]
        )
        e1 = inv1 * b1 + finer(e2)
        mid = e1[1:5, 1:5]
        near = e1[0:4, 1:5] + e1[2:6, 1:5] + e1[1:5, 0:4] + e1[1:5, 2:6] + beside_z(mid, 2)
        e1 = 0.3 * mid + inv1[1:5, 1:5] * (b1[1:5, 1:5] + 2.0 * near)
        e0 = e0_ref[1:9, 1:9] + finer(e1)
        mid = e0[1:7, 1:7]
        near = e0[0:6, 1:7] + e0[2:8, 1:7] + e0[1:7, 0:6] + e0[1:7, 2:8] + beside_z(mid, 1)
        field[...] = 0.3 * mid + inv0[2:8, 2:8] * (rhs[2:8, 2:8] + near)

    for i, d in enumerate(NEAR):
        got = first_in[i]
        arrived(got, 0, i)
        sx, sy = box(first_place, d)
        rhs0[sx, sy] = got[:, :, 0:3, :]
        mass[sx, sy] = got[:, :, 3:4, :]
    inv0[...] = 0.7 / (jnp.broadcast_to(mass[...], inv0.shape) + 6.0)
    inv0[0:3] = inv0[0:3] * inside[0][0]
    inv0[7:10] = inv0[7:10] * inside[0][1]
    inv0[:, 0:3] = inv0[:, 0:3] * inside[1][0]
    inv0[:, 7:10] = inv0[:, 7:10] * inside[1][1]
    multigrid(0, rhs0, z_ref)
    particles(z_ref, part0)
    for i, d in enumerate(NEAR):
        sx, sy = box(wide_cut, d)
        send(part0.at[sx, sy], wide_in[other(d)], 3, i, d)

    def kept(d):
        keep = jnp.bool_(True)
        if d[0]:
            keep = keep & ((gx > 0) if d[0] < 0 else (gx < n_gx - 1))
        if d[1]:
            keep = keep & ((gy > 0) if d[1] < 0 else (gy < n_gy - 1))
        return jnp.where(keep, 1.0, 0.0).astype(F32)

    rhs1[...] = jnp.zeros_like(rhs1)
    rhs1[2:8, 2:8] = part0[...]
    for i, d in enumerate(NEAR):
        got = wide_in[i]
        arrived(got, 3, i)
        sx, sy = box(wide_place, d)
        rhs1[sx, sy] = rhs1[sx, sy] + got[...] * kept(d)
    multigrid(1, rhs1, u_ref)
    energy = particles(u_ref, part1)
    for i, d in enumerate(NEAR):
        sx, sy = box(thin_cut, d)
        send(part1.at[sx, sy], thin_in[other(d)], 4, i, d)

    b = rhs0[3:7, 3:7]
    w = rhs1[3:7, 3:7]
    z = z_ref[1:5, 1:5]
    u = u_ref[1:5, 1:5]
    own_mass = jnp.broadcast_to(mass[3:7, 3:7], z.shape)

    def down(v):
        return jnp.sum(v.sum(axis=(0, 1)), axis=0, keepdims=True)

    sums[...] = jnp.zeros_like(sums)
    sums[0:1] = down(b * z)
    sums[1:2] = down(z * w)
    sums[2:3] = down(b * u)
    sums[3:4] = down(w * u)
    sums[4:5] = down(own_mass * u * u) + jnp.sum(energy, axis=0, keepdims=True)
    across = jnp.broadcast_to(jnp.sum(sums[...], axis=1, keepdims=True), (8, LANES))
    sum_own[...] = jnp.sum(jnp.where(lane2 == sub2, across, 0.0), axis=0, keepdims=True)

    def along(src, slots, stage, count, step):
        for d in range(1, count):
            copy = pltpu.make_async_remote_copy(
                src_ref=src,
                dst_ref=slots.at[d - 1],
                send_sem=line_send.at[stage],
                recv_sem=line_recv.at[stage],
                device_id=device(*step(d)),
                device_id_type=MESH,
            )
            copy.start()
        whole = slots.at[pl.ds(0, count - 1)]
        pltpu.make_async_copy(whole, whole, line_recv.at[stage]).wait()
        total = src[...]
        for d in range(1, count):
            total = total + slots[d - 1]
        return total

    sum_own2[...] = along(sum_own, line_in, 0, n_gx, lambda d: (d, 0))
    total = along(sum_own2, line_in2, 1, n_gy, lambda d: (0, d))

    def scalar(i):
        index = jnp.full((8, LANES), i, jnp.int32)
        return jnp.take_along_axis(
            jnp.broadcast_to(total, (8, LANES)), index, axis=1, mode="promise_in_bounds"
        )

    bz, zw, bu, wu, uv = (scalar(i) for i in range(5))
    step0 = bz / zw
    rz1 = bz - step0 * (bu + zw) + step0 * step0 * wu
    ratio = rz1 / bz
    mixed = zw - step0 * wu
    curve = zw - 2.0 * step0 * wu + step0 * step0 * uv + 2.0 * ratio * mixed + ratio * ratio * zw
    step1 = rz1 / curve
    first = (step0 + step1 + step1 * ratio)[0:3]
    second = (step1 * step0)[0:3]

    x_ref[...] = first * z - second * u
    r_ref[...] = part1[1:5, 1:5]
    for i, d in enumerate(NEAR):
        got = thin_in[i]
        arrived(got, 4, i)
        sx, sy = box(thin_place, d)
        r_ref[sx, sy] = r_ref[sx, sy] + got[...] * kept(d)
    r_ref[...] = b - first * w + second * r_ref[...]

    for copy in started:
        copy.wait_send()
    for turn_no, slots in enumerate((far_in0, far_in1)):
        whole = slots.at[pl.ds(0, len(FAR))]
        pltpu.make_async_copy(whole, whole, far_send.at[turn_no]).wait()
    for stage, (slots, count) in enumerate(((line_in, n_gx), (line_in2, n_gy))):
        whole = slots.at[pl.ds(0, count - 1)]
        pltpu.make_async_copy(whole, whole, line_send.at[stage]).wait()


def solution(mesh):
    n_gx, n_gy = mesh.shape["gx"], mesh.shape["gy"]

    def vmem(*shape, dtype=F32):
        return pltpu.VMEM(shape, dtype)

    scratch = [vmem(*extent(first_cut, (-d[0], -d[1]), 4)) for d in NEAR]
    scratch += [vmem(*extent(wide_cut, (-d[0], -d[1]), 3)) for d in NEAR]
    scratch += [vmem(*extent(thin_cut, (-d[0], -d[1]), 3)) for d in NEAR]
    scratch += [vmem(2, 2, 4, LANES) for _ in range(16)]
    scratch += [
        vmem(3, 4, 4, LANES), vmem(4, 4, LANES), vmem(8, 3, 27, LANES),
        vmem(8, LANES), vmem(8, LANES, dtype=jnp.int32), vmem(8, LANES, dtype=jnp.int32),
    ]
    scratch += [
        vmem(81, 8, LANES),
        vmem(4, 4, 4, LANES),
        vmem(10, 10, 3, LANES),
        vmem(10, 10, 3, LANES),
        vmem(10, 10, 1, LANES),
        vmem(10, 10, 3, LANES),
        vmem(10, 10, 3, LANES),
        vmem(2, 2, 4, LANES),
        vmem(2, 2, 4, LANES),
        vmem(6, 6, 3, LANES),
        vmem(6, 6, 3, LANES),
        vmem(1, LANES),
        vmem(1, LANES),
        vmem(81, 1, LANES),
        vmem(81, 1, LANES),
        vmem(9, 16, LANES),
        vmem(9, 16, LANES),
        vmem(3, 16, LANES),
        vmem(6, 6, 3, LANES),
        vmem(6, 6, 3, LANES),
        vmem(3, 6, 6, 3, LANES),
        vmem(3 * ROWS, 8, LANES),
        vmem(3 * ROWS, 8 * LANES, dtype=BF16),
        vmem(3 * ROWS, 8 * LANES, dtype=BF16),
        vmem(LANES, 8 * LANES, dtype=BF16),
        vmem(ROWS, LANES),
        vmem(6, 6, 3, LANES),
        vmem(6, 6, 3, LANES),
        vmem(8, LANES),
        vmem(1, LANES),
        vmem(1, LANES),
        vmem(n_gx, 1, LANES),
        vmem(n_gy, 1, LANES),
        pltpu.SemaphoreType.DMA((5, 8)),
        pltpu.SemaphoreType.DMA((5, 8)),
        pltpu.SemaphoreType.DMA((2,)),
        pltpu.SemaphoreType.DMA((2,)),
        pltpu.SemaphoreType.DMA((2,)),
        pltpu.SemaphoreType.DMA((2,)),
        pltpu.SemaphoreType.DMA((6,)),
    ]

    def body(*args):
        call = pl.pallas_call(
            lambda *refs: kernel(n_gx, n_gy, *refs),
            out_shape=[jax.ShapeDtypeStruct((4, 4, 3, LANES), F32)] * 2,
            in_specs=[pl.BlockSpec(memory_space=pl.ANY)] * 6,
            out_specs=[pl.BlockSpec(memory_space=pltpu.VMEM)] * 2,
            scratch_shapes=scratch,
            compiler_params=pltpu.CompilerParams(collective_id=0, has_side_effects=True),
            name="cg",
        )
        return tuple(jnp.transpose(v, (2, 0, 1, 3)) for v in call(*args))

    field = P(None, "gx", "gy", None)
    block = P("gx", "gy", None, None)
    return jax.shard_map(
        body,
        mesh=mesh,
        in_specs=(field, P("gx", "gy", None), P("gx", "gy", None, None, None, None)) + (block,) * 3,
        out_specs=(field, field),
        check_vma=False,
    )
```

time: 742 us -> 70.8 us (0.10)
  the two profiles are of different devices: /device:TPU:2 before, /device:TPU:1 now
where the time goes in v1:
time: 70.8 us; the launch traced here: 70.6 us
  Pallas kernels  66.1 us (93%)
  local copies, waits for them, and re-layouts  3.79 us (5%)
    pallas_call x1, Pallas kernels, body(): return tuple((jnp.transpose(v, (2, 0, 1, 3)) for v in call(*args)))  66.1 us
    unnamed x5, local copies, waits for them, and re-layouts  3.79 us

profile of v1, /device:TPU:1, one launch (start us, length us, event | category | flops | bytes accessed | tf_op | source)
XLA Modules:
  0.0 70.6 jit_solution(13611613408435236907)
XLA Ops:
  0.6 1.8 %copy.8.refs_2_ = f32[1,1,8,3,27,128]{5,4,3,2,1,0:T(8,128)} copy(f32[1,1,8,3,27,128]{5,2,4,3,1,0:T(8,128)} %param.8) | data formatting | bytes 663552 | tf_op args[2]
  2.4 66.1 %cg.1 = (f32[4,4,3,128]{3,2,1,0:T(4,128)}, f32[4,4,3,128]{3,2,1,0:T(4,128)}) custom-call(f32[3,4,4,128]{3,2,1,0:T(4,128)} %refs_0_.1, f32[4,4,128]{2,1,0:T(4,128)} %refs_1_.1, f32[1,1,8,3,27,128]{5,4,3,2,1,0:T(8,128)} %copy.8.refs_2_, f32[1,1,8,128]{3,2,1,0:T(8,128)} %refs_3_.1, s32[1,1,8,128]{3,2,1,0:T(8,128)} %refs_4_.1, s32[1,1,8,128]{3,2,1,0:T(8,128)} %refs_5_.1), custom_call_target="tpu_custom_call" | custom-call | tf_op jit(solution)/shard_map/cg/pallas_call | solution.py:587
  68.6 0.0 copy-start
  68.6 1.4 %copy.9 = f32[3,4,4,128]{3,2,1,0:T(4,128)} copy(f32[3,4,4,128]{3,0,2,1:T(4,128)} %bitcast.3) | data formatting | bytes 49152
  69.9 0.0 copy-done
  69.9 0.6 copy.10
Async XLA Ops:
  68.6 1.4 %copy-start = (f32[4,4,3,128]{3,2,1,0:T(4,128)S(1)}, f32[4,4,3,128]{3,2,1,0:T(4,128)}, u32[]{:S(2)}) copy-start(f32[4,4,3,128]{3,2,1,0:T(4,128)} %get-tuple-element.5) | copy-start | bytes 73732

commit v2 on v1

--- a/solution.py
+++ b/solution.py
@@ -25,6 +25,13 @@
         key=lambda d: -abs(d[0]) - abs(d[1]),
     )
 )
+GREETED = tuple(
+    (dx, dy)
+    for dx in range(-3, 4)
+    for dy in range(-3, 4)
+    if 0 < abs(dx) + abs(dy) <= 3
+) + tuple((d, 0) for d in (14, 15, 16, -15, -14))
+CORNER = tuple((p, q) for p in range(4) for q in range(4) if p + q <= 3)
 ROWS = 112
 
 
@@ -73,12 +80,12 @@
     (b_hbm, m_hbm, g_hbm, s_hbm, v_hbm, n_hbm, x_ref, r_ref), refs = refs[:8], refs[8:]
     first_in, wide_in, thin_in = refs[:8], refs[8:16], refs[16:24]
     one_in = (refs[24:32], refs[32:40])
-    (b_in, m_in, g_in, s_in, v_in, n_in), refs = refs[40:46], refs[46:]
+    (b_in, m_in, s_in, v_in, n_in), refs = refs[40:45], refs[45:]
     (
         grad, own, rhs0, rhs1, mass, inv0, e0_ref, one_own0, one_own1, one_rhs, one_inv,
         far_own0, far_own1, far_in0, far_in1, far_rhs, far_inv, far_est, z_ref, u_ref,
         z_shift, f_rows, lhs_hi, lhs_lo, hot, rows_out, part0, part1, sums, sum_own,
-        sum_own2, line_in, line_in2, near_send, near_recv, far_send, far_recv,
+        sum_own2, line_in, line_in2, answer, corner_out, near_send, near_recv, far_send, far_recv,
         line_send, line_recv, local_sem,
     ) = refs
 
@@ -91,16 +98,14 @@
         pltpu.make_async_copy(src, dst, local_sem.at[i])
         for i, (src, dst) in enumerate(
             (
-                (b_hbm, b_in), (m_hbm, m_in), (g_hbm.at[0, 0], g_in),
+                (b_hbm, b_in), (m_hbm, m_in), (g_hbm, grad),
                 (s_hbm.at[0, 0], s_in), (v_hbm.at[0, 0], v_in), (n_hbm.at[0, 0], n_in),
             )
         )
     ]
     for load in loads:
         load.start()
-    partners = {(dx % n_gx, dy % n_gy) for dx, dy in FAR}
-    partners |= {(d, 0) for d in range(1, n_gx)} | {(0, d) for d in range(1, n_gy)}
-    partners = sorted(partners)
+    partners = sorted({(dx % n_gx, dy % n_gy) for dx, dy in GREETED})
     barrier = pltpu.get_barrier_semaphore()
     for dx, dy in partners:
         pl.semaphore_signal(barrier, inc=1, device_id=device(dx, dy), device_id_type=MESH)
@@ -117,6 +122,13 @@
     pl.semaphore_wait(barrier, len(partners))
 
     started = []
+    closers = []
+
+    def close():
+        for copy in started:
+            copy.wait_send()
+        for whole, sem in closers:
+            pltpu.make_async_copy(whole, whole, sem).wait()
 
     def send(src, dst, group, i, d):
         copy = pltpu.make_async_remote_copy(
@@ -137,7 +149,7 @@
         return NEAR.index((-d[0], -d[1]))
 
     for i, d in enumerate(NEAR):
-        sx, sy = box(lambda *a: first_cut(*a), d)
+        sx, sy = box(first_cut, d)
         send(own.at[sx, sy], first_in[other(d)], 0, i, d)
 
     lane4 = lax.broadcasted_iota(jnp.int32, (1, 1, 3, LANES), 3)
@@ -183,8 +195,6 @@
 
     for load in loads[2:]:
         load.wait()
-    for t in range(81):
-        grad[t] = g_in[:, t // 27, t % 27, :]
     node = n_in[...]
     quotient = (node * 2017) >> 18
     k_index = node - quotient * 130
@@ -198,7 +208,7 @@
     shear = effective * (0.5 / (1.0 + POISSON))
     lame = effective * (POISSON / ((1.0 + POISSON) * (1.0 - 2.0 * POISSON)))
 
-    def particles(field, part):
+    def strains(field):
         v = field[...]
         z_shift[0] = turn(v, 1) * low_ok[1]
         z_shift[1] = v
@@ -243,8 +253,9 @@
             for m in range(3)
             for l in range(3)
         ]
-        energy = sum(stress[q] * disp[q] for q in range(9))
-
+        return stress, sum(stress[q] * disp[q] for q in range(9))
+
+    def forces(stress, field, part):
         def scatter(c, carry):
             for m in range(3):
                 spread = []
@@ -265,7 +276,8 @@
                     )
                 for x in range(6):
                     for y in range(6):
-                        f_rows[c * ROWS + (x * 6 + y) * 3 + m] = sum(
+                        row = pl.multiple_of((c * ROWS + (x * 6 + y) * 3 + m) * 8, 8)
+                        f_rows[pl.ds(row, 8), :] = sum(
                             jnp.where(i_index == x - a, spread[a][y], 0.0)
                             for a in range(3)
                             if 0 <= x - a <= 3
@@ -274,7 +286,7 @@
 
         lax.fori_loop(0, 3, scatter, 0)
         for s in range(8):
-            rows = f_rows[:, s, :]
+            rows = f_rows[pl.ds(s, 3 * ROWS, stride=8), :]
             high = rows.astype(BF16)
             lhs_hi[:, s * LANES : (s + 1) * LANES] = high
             lhs_lo[:, s * LANES : (s + 1) * LANES] = (rows - high.astype(F32)).astype(BF16)
@@ -291,9 +303,8 @@
         for n in range(36):
             part[n // 6, n % 6] = rows_out[3 * n : 3 * n + 3, :]
         part[1:5, 1:5] = part[1:5, 1:5] + mass[3:7, 3:7] * field[1:5, 1:5]
-        return energy
-
-    def multigrid(turn_no, rhs, field):
+
+    def multigrid(turn_no, rhs, field, meanwhile):
         one_own = (one_own0, one_own1)[turn_no]
         far_own = (far_own0, far_own1)[turn_no]
         far_slots = (far_in0, far_in1)[turn_no]
@@ -319,8 +330,6 @@
             one_inv[1:5, 4:5] = one_inv[1:5, 4:5] * inside[1][1]
         else:
             one_own[:, :, 3:4, :] = one_own0[:, :, 3:4, :]
-        for i, d in enumerate(NEAR):
-            send(one_own, one_in[turn_no][other(d)], 1 + turn_no, i, d)
         e1 = one_inv[1:5, 1:5] * b1
         r1 = 0.3 * b1[1:3, 1:3] + 2.0 * (
             e1[0:2, 1:3] + e1[2:4, 1:3] + e1[1:3, 0:2] + e1[1:3, 2:4] + beside_z(e1[1:3, 1:3], 2)
@@ -341,6 +350,9 @@
                 device_id_type=MESH,
             )
             copy.start()
+        for i, d in enumerate(NEAR):
+            send(one_own, one_in[turn_no][other(d)], 1 + turn_no, i, d)
+        meanwhile()
         one_rhs[2:4, 2:4] = one_own[:, :, 0:3, :]
         for i, d in enumerate(NEAR):
             got = one_in[turn_no][i]
@@ -356,6 +368,7 @@
                 beside = jnp.broadcast_to(got[:, :, 3:4, :], (2, 2, 3, LANES))
                 one_inv[sx, sy] = (0.7 / (beside + 12.0)) * keep
         far_all = far_slots.at[pl.ds(0, len(FAR))]
+        closers.append((far_all, far_send.at[turn_no]))
         pltpu.make_async_copy(far_all, far_all, far_recv.at[turn_no]).wait()
         for dx, dy in FAR:
             far_rhs[dx + 4, dy + 4 : dy + 5, :] = far_slots[(dx + 4) * 9 + dy + 4]
@@ -405,6 +418,14 @@
         near = e0[0:6, 1:7] + e0[2:8, 1:7] + e0[1:7, 0:6] + e0[1:7, 2:8] + beside_z(mid, 1)
         field[...] = 0.3 * mid + inv0[2:8, 2:8] * (rhs[2:8, 2:8] + near)
 
+    def down(v):
+        return jnp.sum(v.sum(axis=(0, 1)), axis=0, keepdims=True)
+
+    def early_sums():
+        sums[...] = jnp.zeros_like(sums)
+        sums[0:1] = down(rhs0[3:7, 3:7] * z_ref[1:5, 1:5])
+        sums[1:2] = down(rhs1[3:7, 3:7] * z_ref[1:5, 1:5])
+
     for i, d in enumerate(NEAR):
         got = first_in[i]
         arrived(got, 0, i)
@@ -416,11 +437,18 @@
     inv0[7:10] = inv0[7:10] * inside[0][1]
     inv0[:, 0:3] = inv0[:, 0:3] * inside[1][0]
     inv0[:, 7:10] = inv0[:, 7:10] * inside[1][1]
-    multigrid(0, rhs0, z_ref)
-    particles(z_ref, part0)
+    multigrid(0, rhs0, z_ref, lambda: None)
+    stress, _ = strains(z_ref)
+    forces(stress, z_ref, part0)
     for i, d in enumerate(NEAR):
-        sx, sy = box(wide_cut, d)
-        send(part0.at[sx, sy], wide_in[other(d)], 3, i, d)
+        if d[0] and d[1]:
+            n = (2, 3, 4, 5).index(i)
+            for k, (p, q) in enumerate(CORNER):
+                corner_out[n, k] = part0[5 - p if d[0] > 0 else p, 5 - q if d[1] > 0 else q]
+            send(corner_out.at[n], wide_in[other(d)], 3, i, d)
+        else:
+            sx, sy = box(wide_cut, d)
+            send(part0.at[sx, sy], wide_in[other(d)], 3, i, d)
 
     def kept(d):
         keep = jnp.bool_(True)
@@ -435,33 +463,17 @@
     for i, d in enumerate(NEAR):
         got = wide_in[i]
         arrived(got, 3, i)
-        sx, sy = box(wide_place, d)
-        rhs1[sx, sy] = rhs1[sx, sy] + got[...] * kept(d)
-    multigrid(1, rhs1, u_ref)
-    energy = particles(u_ref, part1)
-    for i, d in enumerate(NEAR):
-        sx, sy = box(thin_cut, d)
-        send(part1.at[sx, sy], thin_in[other(d)], 4, i, d)
-
-    b = rhs0[3:7, 3:7]
-    w = rhs1[3:7, 3:7]
-    z = z_ref[1:5, 1:5]
-    u = u_ref[1:5, 1:5]
-    own_mass = jnp.broadcast_to(mass[3:7, 3:7], z.shape)
-
-    def down(v):
-        return jnp.sum(v.sum(axis=(0, 1)), axis=0, keepdims=True)
-
-    sums[...] = jnp.zeros_like(sums)
-    sums[0:1] = down(b * z)
-    sums[1:2] = down(z * w)
-    sums[2:3] = down(b * u)
-    sums[3:4] = down(w * u)
-    sums[4:5] = down(own_mass * u * u) + jnp.sum(energy, axis=0, keepdims=True)
-    across = jnp.broadcast_to(jnp.sum(sums[...], axis=1, keepdims=True), (8, LANES))
-    sum_own[...] = jnp.sum(jnp.where(lane2 == sub2, across, 0.0), axis=0, keepdims=True)
-
-    def along(src, slots, stage, count, step):
+        if d[0] and d[1]:
+            for k, (p, q) in enumerate(CORNER):
+                x, y = (3 - p if d[0] < 0 else 6 + p), (3 - q if d[1] < 0 else 6 + q)
+                rhs1[x, y] = rhs1[x, y] + got[k] * kept(d)
+        else:
+            sx, sy = box(wide_place, d)
+            rhs1[sx, sy] = rhs1[sx, sy] + got[...] * kept(d)
+    multigrid(1, rhs1, u_ref, early_sums)
+    stress, energy = strains(u_ref)
+
+    def line_start(src, slots, stage, count, step):
         for d in range(1, count):
             copy = pltpu.make_async_remote_copy(
                 src_ref=src,
@@ -472,6 +484,9 @@
                 device_id_type=MESH,
             )
             copy.start()
+        closers.append((slots.at[pl.ds(0, count - 1)], line_send.at[stage]))
+
+    def line_end(src, slots, stage, count):
         whole = slots.at[pl.ds(0, count - 1)]
         pltpu.make_async_copy(whole, whole, line_recv.at[stage]).wait()
         total = src[...]
@@ -479,8 +494,24 @@
             total = total + slots[d - 1]
         return total
 
-    sum_own2[...] = along(sum_own, line_in, 0, n_gx, lambda d: (d, 0))
-    total = along(sum_own2, line_in2, 1, n_gy, lambda d: (0, d))
+    b = rhs0[3:7, 3:7]
+    w = rhs1[3:7, 3:7]
+    z = z_ref[1:5, 1:5]
+    u = u_ref[1:5, 1:5]
+    own_mass = jnp.broadcast_to(mass[3:7, 3:7], z.shape)
+    sums[2:3] = down(b * u)
+    sums[3:4] = down(w * u)
+    sums[4:5] = down(own_mass * u * u) + jnp.sum(energy, axis=0, keepdims=True)
+    across = jnp.broadcast_to(jnp.sum(sums[...], axis=1, keepdims=True), (8, LANES))
+    sum_own[...] = jnp.sum(jnp.where(lane2 == sub2, across, 0.0), axis=0, keepdims=True)
+    line_start(sum_own, line_in, 0, n_gx, lambda d: ((16 + d) % n_gx if d != 16 else 16, 0))
+    forces(stress, u_ref, part1)
+    for i, d in enumerate(NEAR):
+        sx, sy = box(thin_cut, d)
+        send(part1.at[sx, sy], thin_in[other(d)], 4, i, d)
+    sum_own2[...] = line_end(sum_own, line_in, 0, n_gx)
+    line_start(sum_own2, line_in2, 1, n_gy, lambda d: (0, (8 + d) % n_gy if d != 8 else 8))
+    total = line_end(sum_own2, line_in2, 1, n_gy)
 
     def scalar(i):
         index = jnp.full((8, LANES), i, jnp.int32)
@@ -498,23 +529,20 @@
     first = (step0 + step1 + step1 * ratio)[0:3]
     second = (step1 * step0)[0:3]
 
-    x_ref[...] = first * z - second * u
-    r_ref[...] = part1[1:5, 1:5]
+    answer[...] = first * z - second * u
+    for n in range(48):
+        x, y, m = n // 12, n // 3 % 4, n % 3
+        x_ref[m, x, y : y + 1, :] = answer[x, y, m : m + 1, :]
+    e0_ref[0:4, 0:4] = part1[1:5, 1:5]
     for i, d in enumerate(NEAR):
-        got = thin_in[i]
-        arrived(got, 4, i)
+        arrived(thin_in[i], 4, i)
         sx, sy = box(thin_place, d)
-        r_ref[sx, sy] = r_ref[sx, sy] + got[...] * kept(d)
-    r_ref[...] = b - first * w + second * r_ref[...]
-
-    for copy in started:
-        copy.wait_send()
-    for turn_no, slots in enumerate((far_in0, far_in1)):
-        whole = slots.at[pl.ds(0, len(FAR))]
-        pltpu.make_async_copy(whole, whole, far_send.at[turn_no]).wait()
-    for stage, (slots, count) in enumerate(((line_in, n_gx), (line_in2, n_gy))):
-        whole = slots.at[pl.ds(0, count - 1)]
-        pltpu.make_async_copy(whole, whole, line_send.at[stage]).wait()
+        e0_ref[sx, sy] = e0_ref[sx, sy] + thin_in[i][...] * kept(d)
+    answer[...] = b - first * w + second * e0_ref[0:4, 0:4]
+    for n in range(48):
+        x, y, m = n // 12, n // 3 % 4, n % 3
+        r_ref[m, x, y : y + 1, :] = answer[x, y, m : m + 1, :]
+    close()
 
 
 def solution(mesh):
@@ -524,11 +552,14 @@
         return pltpu.VMEM(shape, dtype)
 
     scratch = [vmem(*extent(first_cut, (-d[0], -d[1]), 4)) for d in NEAR]
-    scratch += [vmem(*extent(wide_cut, (-d[0], -d[1]), 3)) for d in NEAR]
+    scratch += [
+        vmem(10, 3, LANES) if d[0] and d[1] else vmem(*extent(wide_cut, (-d[0], -d[1]), 3))
+        for d in NEAR
+    ]
     scratch += [vmem(*extent(thin_cut, (-d[0], -d[1]), 3)) for d in NEAR]
     scratch += [vmem(2, 2, 4, LANES) for _ in range(16)]
     scratch += [
-        vmem(3, 4, 4, LANES), vmem(4, 4, LANES), vmem(8, 3, 27, LANES),
+        vmem(3, 4, 4, LANES), vmem(4, 4, LANES),
         vmem(8, LANES), vmem(8, LANES, dtype=jnp.int32), vmem(8, LANES, dtype=jnp.int32),
     ]
     scratch += [
@@ -553,7 +584,7 @@
         vmem(6, 6, 3, LANES),
         vmem(6, 6, 3, LANES),
         vmem(3, 6, 6, 3, LANES),
-        vmem(3 * ROWS, 8, LANES),
+        vmem(3 * ROWS * 8, LANES),
         vmem(3 * ROWS, 8 * LANES, dtype=BF16),
         vmem(3 * ROWS, 8 * LANES, dtype=BF16),
         vmem(LANES, 8 * LANES, dtype=BF16),
@@ -565,6 +596,8 @@
         vmem(1, LANES),
         vmem(n_gx, 1, LANES),
         vmem(n_gy, 1, LANES),
+        vmem(4, 4, 3, LANES),
+        vmem(4, 10, 3, LANES),
         pltpu.SemaphoreType.DMA((5, 8)),
         pltpu.SemaphoreType.DMA((5, 8)),
         pltpu.SemaphoreType.DMA((2,)),
@@ -574,17 +607,19 @@
         pltpu.SemaphoreType.DMA((6,)),
     ]
 
-    def body(*args):
+    def body(right, mass, gradients, *rest):
+        by_tile = jnp.transpose(gradients[0, 0], (1, 2, 0, 3)).reshape(81, 8, LANES)
+        args = (right, mass, by_tile) + rest
         call = pl.pallas_call(
             lambda *refs: kernel(n_gx, n_gy, *refs),
-            out_shape=[jax.ShapeDtypeStruct((4, 4, 3, LANES), F32)] * 2,
+            out_shape=[jax.ShapeDtypeStruct((3, 4, 4, LANES), F32)] * 2,
             in_specs=[pl.BlockSpec(memory_space=pl.ANY)] * 6,
             out_specs=[pl.BlockSpec(memory_space=pltpu.VMEM)] * 2,
             scratch_shapes=scratch,
             compiler_params=pltpu.CompilerParams(collective_id=0, has_side_effects=True),
             name="cg",
         )
-        return tuple(jnp.transpose(v, (2, 0, 1, 3)) for v in call(*args))
+        return tuple(call(*args))
 
     field = P(None, "gx", "gy", None)
     block = P("gx", "gy", None, None)

time: 70.8 us -> 57.3 us (0.81)
  Pallas kernels: 66.1 us -> 54.5 us
  local copies, waits for them, and re-layouts: 3.79 us -> 1.96 us
    pallas_call x1, Pallas kernels: 66.1 us -> 54.5 us  [body(): return tuple(call(*args))]
    unnamed x5 -> x4, local copies, waits for them, and re-layouts: 3.79 us -> 1.96 us
where the time goes in v2:
time: 57.3 us; the launch traced here: 57.1 us
  Pallas kernels  54.5 us (95%)
  local copies, waits for them, and re-layouts  1.96 us (3%)
  between operations  0.65 us (1%)
    pallas_call x1, Pallas kernels, body(): return tuple(call(*args))  54.5 us
    unnamed x4, local copies, waits for them, and re-layouts  1.96 us

profile of v2, /device:TPU:1, one launch (start us, length us, event | category | flops | bytes accessed | tf_op | source)
XLA Modules:
  0.0 57.1 jit_solution(14303340568346166979)
XLA Ops:
  0.6 54.5 %cg.1 = (f32[3,4,4,128]{3,2,1,0:T(4,128)}, f32[3,4,4,128]{3,2,1,0:T(4,128)}) custom-call(f32[3,4,4,128]{3,2,1,0:T(4,128)} %refs_0_.1, f32[4,4,128]{2,1,0:T(4,128)} %refs_1_.1, f32[81,8,128]{2,1,0:T(8,128)} %bitcast.5, f32[1,1,8,128]{3,2,1,0:T(8,128)} %refs_3_.1, s32[1,1,8,128]{3,2,1,0:T(8,128)} %refs_4_.1, s32[1,1,8,128]{3,2,1,0:T(8,128)} %refs_5_.1), custom_call_target="tpu_custom_call" | custom-call | tf_op jit(solution)/shard_map/cg/pallas_call | solution.py:622
  55.1 0.0 copy-start
  55.1 1.4 %copy.10 = f32[3,4,4,128]{3,2,1,0:T(4,128)} copy(f32[3,4,4,128]{3,2,1,0:T(4,128)} %get-tuple-element.4) | data formatting | bytes 49152
  56.5 0.0 copy-done
  56.5 0.6 %copy.11 = f32[3,4,4,128]{3,2,1,0:T(4,128)} copy(f32[3,4,4,128]{3,2,1,0:T(4,128)S(1)} %copy-done) | data formatting | bytes 49152
Async XLA Ops:
  55.1 1.4 %copy-start = (f32[3,4,4,128]{3,2,1,0:T(4,128)S(1)}, f32[3,4,4,128]{3,2,1,0:T(4,128)}, u32[]{:S(2)}) copy-start(f32[3,4,4,128]{3,2,1,0:T(4,128)} %get-tuple-element.5) | copy-start | bytes 73732

commit v3 on v2

--- a/solution.py
+++ b/solution.py
@@ -31,7 +31,7 @@
     for dy in range(-3, 4)
     if 0 < abs(dx) + abs(dy) <= 3
 ) + tuple((d, 0) for d in (14, 15, 16, -15, -14))
-CORNER = tuple((p, q) for p in range(4) for q in range(4) if p + q <= 3)
+CORNER = tuple((p, q) for p in range(3) for q in range(3) if p + q <= 3)
 ROWS = 112
 
 
@@ -50,11 +50,11 @@
 
 
 def wide_cut(d, diagonal):
-    return ((0, 4), (0, 6), (2, 6))[d + 1]
+    return ((0, 3), (0, 6), (3, 6))[d + 1]
 
 
 def wide_place(d, diagonal):
-    return ((0, 4), (2, 8), (6, 10))[d + 1]
+    return ((1, 4), (2, 8), (6, 9))[d + 1]
 
 
 def thin_cut(d, diagonal):
@@ -84,8 +84,8 @@
     (
         grad, own, rhs0, rhs1, mass, inv0, e0_ref, one_own0, one_own1, one_rhs, one_inv,
         far_own0, far_own1, far_in0, far_in1, far_rhs, far_inv, far_est, z_ref, u_ref,
-        z_shift, f_rows, lhs_hi, lhs_lo, hot, rows_out, part0, part1, sums, sum_own,
-        sum_own2, line_in, line_in2, answer, corner_out, near_send, near_recv, far_send, far_recv,
+        z_shift, f_rows, hot, rows_out, part0, part1, sums, sum_own,
+        sum_own2, line_in, line_in2, answer, corner_out, few_out, few_in, one_pad, fine_pad, one_share, mass_rows, inv_rows, near_send, near_recv, far_send, far_recv,
         line_send, line_recv, local_sem,
     ) = refs
 
@@ -105,7 +105,7 @@
     ]
     for load in loads:
         load.start()
-    partners = sorted({(dx % n_gx, dy % n_gy) for dx, dy in GREETED})
+    partners = list(NEAR) + sorted(set(GREETED) - set(NEAR))
     barrier = pltpu.get_barrier_semaphore()
     for dx, dy in partners:
         pl.semaphore_signal(barrier, inc=1, device_id=device(dx, dy), device_id_type=MESH)
@@ -285,16 +285,18 @@
             return carry
 
         lax.fori_loop(0, 3, scatter, 0)
-        for s in range(8):
-            rows = f_rows[pl.ds(s, 3 * ROWS, stride=8), :]
+        contract = (((1,), (1,)), ((), ()))
+        total = None
+        for pair in range(4):
+            rows = jnp.concatenate(
+                [f_rows[pl.ds(2 * pair + q, 3 * ROWS, stride=8), :] for q in range(2)], axis=1
+            )
+            mine = hot[:, 2 * pair * LANES : (2 * pair + 2) * LANES]
             high = rows.astype(BF16)
-            lhs_hi[:, s * LANES : (s + 1) * LANES] = high
-            lhs_lo[:, s * LANES : (s + 1) * LANES] = (rows - high.astype(F32)).astype(BF16)
-        contract = (((1,), (1,)), ((), ()))
-        total = lax.dot_general(lhs_hi[...], hot[...], contract, preferred_element_type=F32)
-        total = total + lax.dot_general(
-            lhs_lo[...], hot[...], contract, preferred_element_type=F32
-        )
+            low = (rows - high.astype(F32)).astype(BF16)
+            for value in (high, low):
+                term = lax.dot_general(value, mine, contract, preferred_element_type=F32)
+                total = term if total is None else total + term
         rows_out[...] = (
             turn(total[0:ROWS], -1) * high_ok[1][0, 0, 0:1]
             + total[ROWS : 2 * ROWS]
@@ -304,12 +306,9 @@
             part[n // 6, n % 6] = rows_out[3 * n : 3 * n + 3, :]
         part[1:5, 1:5] = part[1:5, 1:5] + mass[3:7, 3:7] * field[1:5, 1:5]
 
-    def multigrid(turn_no, rhs, field, meanwhile):
-        one_own = (one_own0, one_own1)[turn_no]
-        far_own = (far_own0, far_own1)[turn_no]
-        far_slots = (far_in0, far_in1)[turn_no]
+    def fine_residual(rhs):
         e0_ref[...] = inv0[...] * rhs[...]
-        r0 = (
+        return (
             0.3 * rhs[1:9, 1:9]
             + e0_ref[0:8, 1:9]
             + e0_ref[2:10, 1:9]
@@ -317,29 +316,10 @@
             + e0_ref[1:9, 2:10]
             + beside_z(e0_ref[1:9, 1:9], 1)
         )
-        b1 = coarser(r0, 1)
-        one_own[:, :, 0:3, :] = b1[1:3, 1:3]
-        if turn_no == 0:
-            mass1 = coarser(jnp.broadcast_to(mass[1:9, 1:9], (8, 8, 3, LANES)), 1)
-            inv1 = 0.7 / (mass1 + 12.0)
-            one_own[:, :, 3:4, :] = mass1[1:3, 1:3, 0:1]
-            one_inv[1:5, 1:5] = inv1
-            one_inv[1:2, 1:5] = one_inv[1:2, 1:5] * inside[0][0]
-            one_inv[4:5, 1:5] = one_inv[4:5, 1:5] * inside[0][1]
-            one_inv[1:5, 1:2] = one_inv[1:5, 1:2] * inside[1][0]
-            one_inv[1:5, 4:5] = one_inv[1:5, 4:5] * inside[1][1]
-        else:
-            one_own[:, :, 3:4, :] = one_own0[:, :, 3:4, :]
-        e1 = one_inv[1:5, 1:5] * b1
-        r1 = 0.3 * b1[1:3, 1:3] + 2.0 * (
-            e1[0:2, 1:3] + e1[2:4, 1:3] + e1[1:3, 0:2] + e1[1:3, 2:4] + beside_z(e1[1:3, 1:3], 2)
-        )
-        b2 = coarser(r1, 2)[0, 0]
-        packed = jnp.sum(b2 * pack_mask, axis=0, keepdims=True)
-        if turn_no == 0:
-            mass2 = coarser(mass1[1:3, 1:3], 2)[0, 0]
-            packed = packed + mass2[0:1] * mass_mask
-        far_own[...] = packed
+
+    def far_start(turn_no):
+        far_own = (far_own0, far_own1)[turn_no]
+        far_slots = (far_in0, far_in1)[turn_no]
         for dx, dy in FAR:
             copy = pltpu.make_async_remote_copy(
                 src_ref=far_own,
@@ -350,9 +330,76 @@
                 device_id_type=MESH,
             )
             copy.start()
+
+    def one_start(turn_no):
         for i, d in enumerate(NEAR):
+            one_own = (one_own0, one_own1)[turn_no]
             send(one_own, one_in[turn_no][other(d)], 1 + turn_no, i, d)
-        meanwhile()
+
+    def first_half():
+        b1 = coarser(fine_residual(rhs0), 1)
+        mass1 = coarser(jnp.broadcast_to(mass[1:9, 1:9], (8, 8, 3, LANES)), 1)
+        inv1 = 0.7 / (mass1 + 12.0)
+        one_inv[1:5, 1:5] = inv1
+        one_inv[1:2, 1:5] = one_inv[1:2, 1:5] * inside[0][0]
+        one_inv[4:5, 1:5] = one_inv[4:5, 1:5] * inside[0][1]
+        one_inv[1:5, 1:2] = one_inv[1:5, 1:2] * inside[1][0]
+        one_inv[1:5, 4:5] = one_inv[1:5, 4:5] * inside[1][1]
+        e1 = one_inv[1:5, 1:5] * b1
+        r1 = 0.3 * b1[1:3, 1:3] + 2.0 * (
+            e1[0:2, 1:3] + e1[2:4, 1:3] + e1[1:3, 0:2] + e1[1:3, 2:4] + beside_z(e1[1:3, 1:3], 2)
+        )
+        b2 = coarser(r1, 2)[0, 0]
+        mass2 = coarser(mass1[1:3, 1:3], 2)[0, 0]
+        far_own0[...] = (
+            jnp.sum(b2 * pack_mask, axis=0, keepdims=True) + mass2[0:1] * mass_mask
+        )
+        far_start(0)
+        one_own0[:, :, 0:3, :] = b1[1:3, 1:3]
+        one_own0[:, :, 3:4, :] = mass1[1:3, 1:3, 0:1]
+        one_start(0)
+        for pad in (fine_pad, one_pad, one_share, rhs1):
+            pad[...] = jnp.zeros_like(pad)
+
+    def own_share():
+        est = inv0[2:8, 2:8] * part0[...]
+        e0_ref[2:8, 2:8] = est
+        fine_pad[1:7, 1:7] = (
+            0.3 * part0[...]
+            + e0_ref[1:7, 2:8]
+            + e0_ref[3:9, 2:8]
+            + e0_ref[2:8, 1:7]
+            + e0_ref[2:8, 3:9]
+            + beside_z(est, 1)
+        )
+        fine_pad[0:1, 1:7] = est[0:1]
+        fine_pad[7:8, 1:7] = est[5:6]
+        fine_pad[1:7, 0:1] = est[:, 0:1]
+        fine_pad[1:7, 7:8] = est[:, 5:6]
+        b1 = coarser(fine_pad[...], 1)
+        est = one_inv[1:5, 1:5] * b1
+        one_pad[1:5, 1:5] = est
+        one_share[1:5, 1:5] = 0.3 * b1 + 2.0 * (
+            one_pad[0:4, 1:5]
+            + one_pad[2:6, 1:5]
+            + one_pad[1:5, 0:4]
+            + one_pad[1:5, 2:6]
+            + beside_z(est, 2)
+        )
+        one_share[0:1, 1:5] = 2.0 * est[0:1]
+        one_share[5:6, 1:5] = 2.0 * est[3:4]
+        one_share[1:5, 0:1] = 2.0 * est[:, 0:1]
+        one_share[1:5, 5:6] = 2.0 * est[:, 3:4]
+        r1 = one_share[...]
+        b2 = coarser(r1, 2)
+        for x in range(3):
+            for y in range(3):
+                few_out[3 * x + y] = jnp.sum(b2[x, y] * pack_mask, axis=0, keepdims=True)
+
+    def second_half(turn_no, rhs, field):
+        far_own = (far_own0, far_own1)[turn_no]
+        far_slots = (far_in0, far_in1)[turn_no]
+        one_own = (one_own0, one_own1)[turn_no]
         one_rhs[2:4, 2:4] = one_own[:, :, 0:3, :]
         for i, d in enumerate(NEAR):
             got = one_in[turn_no][i]
@@ -432,14 +479,35 @@
         sx, sy = box(first_place, d)
         rhs0[sx, sy] = got[:, :, 0:3, :]
         mass[sx, sy] = got[:, :, 3:4, :]
-    inv0[...] = 0.7 / (jnp.broadcast_to(mass[...], inv0.shape) + 6.0)
-    inv0[0:3] = inv0[0:3] * inside[0][0]
-    inv0[7:10] = inv0[7:10] * inside[0][1]
-    inv0[:, 0:3] = inv0[:, 0:3] * inside[1][0]
-    inv0[:, 7:10] = inv0[:, 7:10] * inside[1][1]
-    multigrid(0, rhs0, z_ref, lambda: None)
+    for x in range(10):
+        for y in range(10):
+            mass_rows[x, y : y + 1, :] = mass[x, y]
+    at_x = lax.broadcasted_iota(jnp.int32, (10, 16, LANES), 0) + (gx * 4 - 3)
+    at_y = lax.broadcasted_iota(jnp.int32, (10, 16, LANES), 1) + (gy * 4 - 3)
+    within = (at_x >= 0) & (at_x < 4 * n_gx) & (at_y >= 0) & (at_y < 4 * n_gy)
+    inv_rows[...] = jnp.where(within, 0.7 / (mass_rows[...] + 6.0), 0.0)
+    for x in range(10):
+        for y in range(10):
+            inv0[x, y] = jnp.broadcast_to(inv_rows[x, y : y + 1, :], (3, LANES))
+    first_half()
+    second_half(0, rhs0, z_ref)
+    for x in (1, 8):
+        e0_ref[x : x + 1, 1:9] = jnp.zeros((1, 8, 3, LANES), F32)
+        e0_ref[1:9, x : x + 1] = jnp.zeros((8, 1, 3, LANES), F32)
     stress, _ = strains(z_ref)
     forces(stress, z_ref, part0)
+
+    def kept(d):
+        keep = jnp.bool_(True)
+        if d[0]:
+            keep = keep & ((gx > 0) if d[0] < 0 else (gx < n_gx - 1))
+        if d[1]:
+            keep = keep & ((gy > 0) if d[1] < 0 else (gy < n_gy - 1))
+        return jnp.where(keep, 1.0, 0.0).astype(F32)
+
+    own_share()
+    for i, d in enumerate(NEAR):
+        send(few_out.at[3 * d[0] + d[1] + 4], few_in.at[other(d)], 5, i, d)
     for i, d in enumerate(NEAR):
         if d[0] and d[1]:
             n = (2, 3, 4, 5).index(i)
@@ -449,17 +517,13 @@
         else:
             sx, sy = box(wide_cut, d)
             send(part0.at[sx, sy], wide_in[other(d)], 3, i, d)
-
-    def kept(d):
-        keep = jnp.bool_(True)
-        if d[0]:
-            keep = keep & ((gx > 0) if d[0] < 0 else (gx < n_gx - 1))
-        if d[1]:
-            keep = keep & ((gy > 0) if d[1] < 0 else (gy < n_gy - 1))
-        return jnp.where(keep, 1.0, 0.0).astype(F32)
-
-    rhs1[...] = jnp.zeros_like(rhs1)
     rhs1[2:8, 2:8] = part0[...]
+    coarse = few_out[4]
+    for i, d in enumerate(NEAR):
+        arrived(few_in.at[i], 5, i)
+        coarse = coarse + few_in[i] * kept(d)
+    far_own1[...] = coarse
+    far_start(1)
     for i, d in enumerate(NEAR):
         got = wide_in[i]
         arrived(got, 3, i)
@@ -470,7 +534,19 @@
         else:
             sx, sy = box(wide_place, d)
             rhs1[sx, sy] = rhs1[sx, sy] + got[...] * kept(d)
-    multigrid(1, rhs1, u_ref, early_sums)
+    e0_ref[1:9, 1:9] = inv0[1:9, 1:9] * rhs1[1:9, 1:9]
+    r0 = (
+        0.3 * rhs1[3:7, 3:7]
+        + e0_ref[2:6, 3:7]
+        + e0_ref[4:8, 3:7]
+        + e0_ref[3:7, 2:6]
+        + e0_ref[3:7, 4:8]
+        + beside_z(e0_ref[3:7, 3:7], 1)
+    )
+    one_own1[...] = coarser(r0, 1)
+    one_start(1)
+    early_sums()
+    second_half(1, rhs1, u_ref)
     stress, energy = strains(u_ref)
 
     def line_start(src, slots, stage, count, step):
@@ -553,11 +629,12 @@
 
     scratch = [vmem(*extent(first_cut, (-d[0], -d[1]), 4)) for d in NEAR]
     scratch += [
-        vmem(10, 3, LANES) if d[0] and d[1] else vmem(*extent(wide_cut, (-d[0], -d[1]), 3))
+        vmem(len(CORNER), 3, LANES) if d[0] and d[1] else vmem(*extent(wide_cut, (-d[0], -d[1]), 3))
         for d in NEAR
     ]
     scratch += [vmem(*extent(thin_cut, (-d[0], -d[1]), 3)) for d in NEAR]
-    scratch += [vmem(2, 2, 4, LANES) for _ in range(16)]
+    scratch += [vmem(2, 2, 4, LANES) for _ in range(8)]
+    scratch += [vmem(2, 2, 3, LANES) for _ in range(8)]
     scratch += [
         vmem(3, 4, 4, LANES), vmem(4, 4, LANES),
         vmem(8, LANES), vmem(8, LANES, dtype=jnp.int32), vmem(8, LANES, dtype=jnp.int32),
@@ -571,7 +648,7 @@
         vmem(10, 10, 3, LANES),
         vmem(10, 10, 3, LANES),
         vmem(2, 2, 4, LANES),
-        vmem(2, 2, 4, LANES),
+        vmem(2, 2, 3, LANES),
         vmem(6, 6, 3, LANES),
         vmem(6, 6, 3, LANES),
         vmem(1, LANES),
@@ -585,8 +662,6 @@
         vmem(6, 6, 3, LANES),
         vmem(3, 6, 6, 3, LANES),
         vmem(3 * ROWS * 8, LANES),
-        vmem(3 * ROWS, 8 * LANES, dtype=BF16),
-        vmem(3 * ROWS, 8 * LANES, dtype=BF16),
         vmem(LANES, 8 * LANES, dtype=BF16),
         vmem(ROWS, LANES),
         vmem(6, 6, 3, LANES),
@@ -597,9 +672,16 @@
         vmem(n_gx, 1, LANES),
         vmem(n_gy, 1, LANES),
         vmem(4, 4, 3, LANES),
-        vmem(4, 10, 3, LANES),
-        pltpu.SemaphoreType.DMA((5, 8)),
-        pltpu.SemaphoreType.DMA((5, 8)),
+        vmem(4, len(CORNER), 3, LANES),
+        vmem(9, 1, LANES),
+        vmem(8, 1, LANES),
+        vmem(6, 6, 3, LANES),
+        vmem(8, 8, 3, LANES),
+        vmem(6, 6, 3, LANES),
+        vmem(10, 16, LANES),
+        vmem(10, 16, LANES),
+        pltpu.SemaphoreType.DMA((6, 8)),
+        pltpu.SemaphoreType.DMA((6, 8)),
         pltpu.SemaphoreType.DMA((2,)),
         pltpu.SemaphoreType.DMA((2,)),
         pltpu.SemaphoreType.DMA((2,)),
@@ -612,7 +694,7 @@
         args = (right, mass, by_tile) + rest
         call = pl.pallas_call(
             lambda *refs: kernel(n_gx, n_gy, *refs),
-            out_shape=[jax.ShapeDtypeStruct((3, 4, 4, LANES), F32)] * 2,
+            out_shape=[pltpu.VMEM((3, 4, 4, LANES), F32)] * 2,
             in_specs=[pl.BlockSpec(memory_space=pl.ANY)] * 6,
             out_specs=[pl.BlockSpec(memory_space=pltpu.VMEM)] * 2,
             scratch_shapes=scratch,

time: 57.3 us -> 55.3 us (0.965)
  Pallas kernels: 54.5 us -> 53.3 us
  local copies, waits for them, and re-layouts: 1.96 us -> 1.22 us
    pallas_call x1, Pallas kernels: 54.5 us -> 53.3 us  [body(): return tuple(call(*args))]
    unnamed x4 -> x2, local copies, waits for them, and re-layouts: 1.96 us -> 1.22 us
where the time goes in v3:
time: 55.3 us; the launch traced here: 55.1 us
  Pallas kernels  53.3 us (96%)
  local copies, waits for them, and re-layouts  1.22 us (2%)
  between operations  0.64 us (1%)
    pallas_call x1, Pallas kernels, body(): return tuple(call(*args))  53.3 us
    unnamed x2, local copies, waits for them, and re-layouts  1.22 us

profile of v3, /device:TPU:1, one launch (start us, length us, event | category | flops | bytes accessed | tf_op | source)
XLA Modules:
  0.0 55.1 jit_solution(17686075966484248272)
XLA Ops:
  0.6 53.3 %cg.1 = (f32[3,4,4,128]{3,2,1,0:T(4,128)S(1)}, f32[3,4,4,128]{3,2,1,0:T(4,128)S(1)}) custom-call(f32[3,4,4,128]{3,2,1,0:T(4,128)} %refs_0_.1, f32[4,4,128]{2,1,0:T(4,128)} %refs_1_.1, f32[81,8,128]{2,1,0:T(8,128)} %bitcast.5, f32[1,1,8,128]{3,2,1,0:T(8,128)} %refs_3_.1, s32[1,1,8,128]{3,2,1,0:T(8,128)} %refs_4_.1, s32[1,1,8,128]{3,2,1,0:T(8,128)} %refs_5_.1), custom_call_target="tpu_custom_call" | custom-call | tf_op jit(solution)/shard_map/cg/pallas_call | solution.py:704
  53.9 0.6 %copy.10 = f32[3,4,4,128]{3,2,1,0:T(4,128)} copy(f32[3,4,4,128]{3,2,1,0:T(4,128)S(1)} %get-tuple-element.2) | data formatting | bytes 49152
  54.5 0.6 %copy.11 = f32[3,4,4,128]{3,2,1,0:T(4,128)} copy(f32[3,4,4,128]{3,2,1,0:T(4,128)S(1)} %get-tuple-element.3) | data formatting | bytes 49152

commit v4 on v3

--- a/solution.py
+++ b/solution.py
@@ -14,6 +14,7 @@
     (dx, dy)
     for dx, dy in ((0, 1), (0, -1), (1, 1), (1, -1), (-1, 1), (-1, -1), (1, 0), (-1, 0))
 )
+DIAGONAL_FIRST = tuple(sorted(enumerate(NEAR), key=lambda e: -abs(e[1][0]) - abs(e[1][1])))
 FAR = tuple(
     sorted(
         (
@@ -22,7 +23,7 @@
             for dy in range(-4, 5)
             if (dx, dy) != (0, 0) and max(abs(dx) - 1, 0) + max(abs(dy) - 1, 0) <= 3
         ),
-        key=lambda d: -abs(d[0]) - abs(d[1]),
+        key=lambda d: (-abs(d[1]) - (0, 2, 2, 3, 3)[abs(d[0])], -abs(d[1])),
     )
 )
 GREETED = tuple(
@@ -35,6 +36,10 @@
 ROWS = 112
 
 
+def farthest(n):
+    return sorted(range(1, n), key=lambda d: (-min(d, n - d), d))
+
+
 def first_cut(d, diagonal):
     if d == 0:
         return (0, 4)
@@ -77,7 +82,8 @@
 
 
 def kernel(n_gx, n_gy, *refs):
-    (b_hbm, m_hbm, g_hbm, s_hbm, v_hbm, n_hbm, x_ref, r_ref), refs = refs[:8], refs[8:]
+    (b_hbm, m_hbm, g_hbm, s_hbm, v_hbm, n_hbm, both_ref), refs = refs[:7], refs[7:]
+    x_ref, r_ref = both_ref.at[0], both_ref.at[1]
     first_in, wide_in, thin_in = refs[:8], refs[8:16], refs[16:24]
     one_in = (refs[24:32], refs[32:40])
     (b_in, m_in, s_in, v_in, n_in), refs = refs[40:45], refs[45:]
@@ -148,7 +154,7 @@
     def other(d):
         return NEAR.index((-d[0], -d[1]))
 
-    for i, d in enumerate(NEAR):
+    for i, d in DIAGONAL_FIRST:
         sx, sy = box(first_cut, d)
         send(own.at[sx, sy], first_in[other(d)], 0, i, d)
 
@@ -506,7 +512,7 @@
         return jnp.where(keep, 1.0, 0.0).astype(F32)
 
     own_share()
-    for i, d in enumerate(NEAR):
+    for i, d in DIAGONAL_FIRST:
         send(few_out.at[3 * d[0] + d[1] + 4], few_in.at[other(d)], 5, i, d)
     for i, d in enumerate(NEAR):
         if d[0] and d[1]:
@@ -580,13 +586,13 @@
     sums[4:5] = down(own_mass * u * u) + jnp.sum(energy, axis=0, keepdims=True)
     across = jnp.broadcast_to(jnp.sum(sums[...], axis=1, keepdims=True), (8, LANES))
     sum_own[...] = jnp.sum(jnp.where(lane2 == sub2, across, 0.0), axis=0, keepdims=True)
-    line_start(sum_own, line_in, 0, n_gx, lambda d: ((16 + d) % n_gx if d != 16 else 16, 0))
+    line_start(sum_own, line_in, 0, n_gx, lambda d: (farthest(n_gx)[d - 1], 0))
     forces(stress, u_ref, part1)
     for i, d in enumerate(NEAR):
         sx, sy = box(thin_cut, d)
         send(part1.at[sx, sy], thin_in[other(d)], 4, i, d)
     sum_own2[...] = line_end(sum_own, line_in, 0, n_gx)
-    line_start(sum_own2, line_in2, 1, n_gy, lambda d: (0, (8 + d) % n_gy if d != 8 else 8))
+    line_start(sum_own2, line_in2, 1, n_gy, lambda d: (0, farthest(n_gy)[d - 1]))
     total = line_end(sum_own2, line_in2, 1, n_gy)
 
     def scalar(i):
@@ -694,14 +700,15 @@
         args = (right, mass, by_tile) + rest
         call = pl.pallas_call(
             lambda *refs: kernel(n_gx, n_gy, *refs),
-            out_shape=[pltpu.VMEM((3, 4, 4, LANES), F32)] * 2,
+            out_shape=pltpu.VMEM((2, 3, 4, 4, LANES), F32),
             in_specs=[pl.BlockSpec(memory_space=pl.ANY)] * 6,
-            out_specs=[pl.BlockSpec(memory_space=pltpu.VMEM)] * 2,
+            out_specs=pl.BlockSpec(memory_space=pltpu.VMEM),
             scratch_shapes=scratch,
             compiler_params=pltpu.CompilerParams(collective_id=0, has_side_effects=True),
             name="cg",
         )
-        return tuple(call(*args))
+        both = call(*args)
+        return both[0], both[1]
 
     field = P(None, "gx", "gy", None)
     block = P("gx", "gy", None, None)

time: 55.3 us -> 54.7 us (0.989)
  local copies, waits for them, and re-layouts: 1.22 us -> 0.62 us
    unnamed x2 -> x0, local copies, waits for them, and re-layouts: 1.22 us -> none
    squeeze x0 -> x1, local copies, waits for them, and re-layouts: none -> 0.62 us  [body(): return (both[0], both[1])]
where the time goes in v4:
time: 54.7 us; the launch traced here: 54.5 us
  Pallas kernels  53.3 us (97%)
  between operations  0.64 us (1%)
  local copies, waits for them, and re-layouts  0.62 us (1%)
    pallas_call x1, Pallas kernels, body(): both = call(*args)  53.3 us

profile of v4, /device:TPU:1, one launch (start us, length us, event | category | flops | bytes accessed | tf_op | source)
XLA Modules:
  0.0 54.5 jit_solution(7587433910019525164)
XLA Ops:
  0.6 53.3 %cg.1 = f32[2,3,4,4,128]{4,3,2,1,0:T(4,128)S(1)} custom-call(f32[3,4,4,128]{3,2,1,0:T(4,128)} %refs_0_.1, f32[4,4,128]{2,1,0:T(4,128)} %refs_1_.1, f32[81,8,128]{2,1,0:T(8,128)} %bitcast.9, f32[1,1,8,128]{3,2,1,0:T(8,128)} %refs_3_.1, s32[1,1,8,128]{3,2,1,0:T(8,128)} %refs_4_.1, s32[1,1,8,128]{3,2,1,0:T(8,128)} %refs_5_.1), custom_call_target="tpu_custom_call" | custom-call | tf_op jit(solution)/shard_map/cg/pallas_call | solution.py:710
  53.9 0.6 %slice_bitcast_fusion = (f32[3,4,4,128]{3,2,1,0:T(4,128)}, f32[3,4,4,128]{3,2,1,0:T(4,128)}) fusion(f32[2,3,4,4,128]{4,3,2,1,0:T(4,128)S(1)} %cg.1), kind=kLoop, calls=%fused_computation | loop fusion | bytes 98304 | tf_op jit(solution)/shard_map/squeeze | solution.py:711

commit v5 on v4

--- a/solution.py
+++ b/solution.py
@@ -89,7 +89,7 @@
     (b_in, m_in, s_in, v_in, n_in), refs = refs[40:45], refs[45:]
     (
         grad, own, rhs0, rhs1, mass, inv0, e0_ref, one_own0, one_own1, one_rhs, one_inv,
-        far_own0, far_own1, far_in0, far_in1, far_rhs, far_inv, far_est, z_ref, u_ref,
+        far_own0, far_own1, far_in0, far_in1, far_inv, far_est, z_ref, u_ref,
         z_shift, f_rows, hot, rows_out, part0, part1, sums, sum_own,
         sum_own2, line_in, line_in2, answer, corner_out, few_out, few_in, one_pad, fine_pad, one_share, mass_rows, inv_rows, near_send, near_recv, far_send, far_recv,
         line_send, line_recv, local_sem,
@@ -329,7 +329,7 @@
         for dx, dy in FAR:
             copy = pltpu.make_async_remote_copy(
                 src_ref=far_own,
-                dst_ref=far_slots.at[(4 - dx) * 9 + 4 - dy],
+                dst_ref=far_slots.at[4 - dx, pl.ds(4 - dy, 1), :],
                 send_sem=far_send.at[turn_no],
                 recv_sem=far_recv.at[turn_no],
                 device_id=device(dx, dy),
@@ -420,13 +420,11 @@
                     keep = keep * inside[1][(d[1] + 1) // 2]
                 beside = jnp.broadcast_to(got[:, :, 3:4, :], (2, 2, 3, LANES))
                 one_inv[sx, sy] = (0.7 / (beside + 12.0)) * keep
-        far_all = far_slots.at[pl.ds(0, len(FAR))]
+        far_all = far_slots.at[pl.ds(0, 7), pl.ds(0, 8), :]
         closers.append((far_all, far_send.at[turn_no]))
         pltpu.make_async_copy(far_all, far_all, far_recv.at[turn_no]).wait()
-        for dx, dy in FAR:
-            far_rhs[dx + 4, dy + 4 : dy + 5, :] = far_slots[(dx + 4) * 9 + dy + 4]
-        far_rhs[4, 4:5, :] = far_own[...]
-        b = far_rhs[...]
+        far_slots[4, 4:5, :] = far_own[...]
+        b = far_slots[...]
         if turn_no == 0:
             quarter = lax.broadcasted_iota(jnp.int32, b.shape, 2) & 3
             diagonal = jnp.where(
@@ -659,8 +657,7 @@
         vmem(6, 6, 3, LANES),
         vmem(1, LANES),
         vmem(1, LANES),
-        vmem(81, 1, LANES),
-        vmem(81, 1, LANES),
+        vmem(9, 16, LANES),
         vmem(9, 16, LANES),
         vmem(9, 16, LANES),
         vmem(3, 16, LANES),

time: 54.7 us -> 54.5 us (level)
  no operation moved by 1% of the time
where the time goes in v5:
time: 54.5 us; the launch traced here: 54.4 us
  Pallas kernels  53.1 us (97%)
  between operations  0.64 us (1%)
  local copies, waits for them, and re-layouts  0.62 us (1%)
    pallas_call x1, Pallas kernels, body(): both = call(*args)  53.1 us

profile of v5, /device:TPU:1, one launch (start us, length us, event | category | flops | bytes accessed | tf_op | source)
XLA Modules:
  0.0 54.4 jit_solution(2388138116864811929)
XLA Ops:
  0.6 53.1 %cg.1 = f32[2,3,4,4,128]{4,3,2,1,0:T(4,128)S(1)} custom-call(f32[3,4,4,128]{3,2,1,0:T(4,128)} %refs_0_.1, f32[4,4,128]{2,1,0:T(4,128)} %refs_1_.1, f32[81,8,128]{2,1,0:T(8,128)} %bitcast.9, f32[1,1,8,128]{3,2,1,0:T(8,128)} %refs_3_.1, s32[1,1,8,128]{3,2,1,0:T(8,128)} %refs_4_.1, s32[1,1,8,128]{3,2,1,0:T(8,128)} %refs_5_.1), custom_call_target="tpu_custom_call" | custom-call | tf_op jit(solution)/shard_map/cg/pallas_call | solution.py:707
  53.8 0.6 %slice_bitcast_fusion = (f32[3,4,4,128]{3,2,1,0:T(4,128)}, f32[3,4,4,128]{3,2,1,0:T(4,128)}) fusion(f32[2,3,4,4,128]{4,3,2,1,0:T(4,128)S(1)} %cg.1), kind=kLoop, calls=%fused_computation | loop fusion | bytes 98304 | tf_op jit(solution)/shard_map/squeeze | solution.py:708
